TPU v7x, 128 devices: a whole 4x4x4 slice. The times are simulated.
128 devices in a mesh: view: 4 (over x), xy: 16 (over z, y), gz: 2 (over core).
Axes of the slice: x: 4, y: 4, z: 4, core: 2. Of those that a mesh axis runs over, the one named last changes fastest.
Arguments:
- estimate: float32 [64, 1024, 128], P('gz', 'xy'), may hold values from 0.5 to 2
- views: bfloat16 [4, 64, 1024, 128], P('view', 'gz', 'xy'), may hold values from 0.19921875 to 3
- shifts: int32 [4, 3], P('view'), may hold values from -32 to 32, as said below
- kernels: float32 [4, 3, 63], P('view'), may hold values from 0.02 to 1
- coverage: int32 [4, 8, 1], replicated, may hold values from 0 to 1, as said below
Outputs:
- refined: float32 [64, 1024, 128], P('gz', 'xy')
Inputs may be any that keep to these rules, and one draw needn't show every extreme that they name: `shifts`: both ends -32 and 32 occur in every draw. `coverage`: every block is covered by at least one view.
All inputs are finite; a program needn't handle non-finite values.
Results may differ from a plain program's by a relative error of at most 0.0003.
Values may be sent and summed in bfloat16 or wider, within the bound.
No kernel may reach another device: no remote copies, remote signals or barrier semaphores. Data moves between devices by JAX's collectives and lax.ppermute only.
A program may use at most 64 MiB of HBM per device.

v0:
```python
import jax
import jax.numpy as jnp
from jax import lax
from jax.experimental import pallas as pl
from jax.experimental.pallas import tpu as pltpu
from jax.sharding import PartitionSpec as P


F32 = jnp.float32
BF16 = jnp.bfloat16
F16 = jnp.float16
ITERS = 2
VIEWS = 4
PLANES = 64
ROWS = 32
WIDTH = 128
SPAN = 3 * ROWS
QUARTER = ROWS // VIEWS
FLAT = ROWS * PLANES
QFLAT = QUARTER * PLANES
HALF = 31
SHIFT = 32
CHUNK = 512
TAIL = 8
BLOCK = 128
STRIPS = ("xy", "gz")


def dot(a, b):
    return jnp.dot(a, b, preferred_element_type=F32)


def split(x):
    high = x.astype(BF16)
    return high, (x - high.astype(F32)).astype(BF16)


def call(kernel, outs, scratch=(), flops=10**8, smem=()):
    def space(i):
        return pltpu.SMEM if i in smem else pltpu.VMEM

    def run(*args):
        specs = [pl.BlockSpec(memory_space=space(i)) for i in range(len(args))]
        one = not isinstance(outs, (list, tuple))
        shapes = [outs] if one else list(outs)
        made = pl.pallas_call(
            kernel,
            out_shape=shapes,
            in_specs=specs,
            out_specs=[pl.BlockSpec(memory_space=pltpu.VMEM)] * len(shapes),
            scratch_shapes=list(scratch),
            compiler_params=pltpu.CompilerParams(vmem_limit_bytes=16 << 20),
            cost_estimate=pl.CostEstimate(flops=flops, bytes_accessed=4 << 20, transcendentals=0),
        )(*args)
        return made[0] if one else made

    return run


def loop(count, body):
    for c in range(count):
        body(c)


def arr(shape, dtype):
    return jax.ShapeDtypeStruct(shape, dtype)


def strip_index():
    return lax.axis_index("xy") * 2 + lax.axis_index("gz")


def prep_estimate_kernel(est, eb, em, eo, mine, theirs):
    v, g = lax.axis_index("view"), lax.axis_index("gz")
    eb[...] = est[...].astype(BF16)

    @pl.when(g == 0)
    def _():
        em[...] = est[:, 0:ROWS, :].astype(BF16)
        eo[...] = est[:, ROWS : 2 * ROWS, :].astype(BF16)

    @pl.when(g == 1)
    def _():
        eo[...] = est[:, 0:ROWS, :].astype(BF16)
        em[...] = est[:, ROWS : 2 * ROWS, :].astype(BF16)

    here = pl.multiple_of(g * ROWS + v * QUARTER, QUARTER)
    there = pl.multiple_of((1 - g) * ROWS + v * QUARTER, QUARTER)
    mine[...] = est[:, pl.ds(here, QUARTER), :]
    theirs[...] = est[:, pl.ds(there, QUARTER), :]


def prep_views_kernel(views, vm, vo):
    g = lax.axis_index("gz")

    @pl.when(g == 0)
    def _():
        vm[...] = views[0, :, 0:ROWS, :]
        vo[...] = views[0, :, ROWS : 2 * ROWS, :]

    @pl.when(g == 1)
    def _():
        vo[...] = views[0, :, 0:ROWS, :]
        vm[...] = views[0, :, ROWS : 2 * ROWS, :]


def toeplitz(row, rows, shift):
    return pltpu.roll(jnp.broadcast_to(row, (rows, WIDTH)), shift, 1, stride=1, stride_axis=0)


def normed(taps):
    return taps / jnp.sum(taps, axis=1, keepdims=True)


def x_matrix(row):
    i = lax.broadcasted_iota(jnp.int32, (WIDTH, WIDTH), 0)
    j = lax.broadcasted_iota(jnp.int32, (WIDTH, WIDTH), 1)
    full = toeplitz(row, WIDTH, WIDTH - HALF)
    return jnp.where(jnp.abs(i - j) <= HALF, full, 0.0)


def row_valid(rows):
    r = strip_index()
    j = lax.broadcasted_iota(jnp.int32, (rows, WIDTH), 1)
    low = jnp.where(r == 0, ROWS, 0)
    high = jnp.where(r == 2 * lax.axis_size("xy") - 1, 2 * ROWS, SPAN)
    return (j >= low) & (j < high)


def own_mats_kernel(taps, shifts, yw, yf, yb, zf, x1f, x2f, yd, xd):
    k = normed(taps[...])
    valid = row_valid(ROWS)
    column = lax.broadcasted_iota(jnp.int32, (ROWS, WIDTH), 1)
    kept = (lax.axis_index("gz") == 0) | ((column >= ROWS) & (column < 2 * ROWS))

    def sides(y):
        return jnp.where(kept, y, pltpu.roll(y, 2 * ROWS, 1))

    forward = jnp.where(valid, toeplitz(k[1:2], ROWS, 1), 0.0)
    backward = jnp.where(valid, toeplitz(k[4:5], ROWS, 1), 0.0)
    for ref, y in ((yw, forward), (yf, sides(forward)), (yb, sides(backward))):
        h, l = split(y)
        ref[0:ROWS, :] = h
        ref[ROWS : 2 * ROWS, :] = l
    lane = lax.broadcasted_iota(jnp.int32, (PLANES, WIDTH), 1)
    z = jnp.where(lane < PLANES, toeplitz(k[0:1], PLANES, WIDTH - HALF), 0.0)
    zh = z.astype(BF16).astype(F32)
    zf[0:PLANES, :] = (zh + pltpu.roll(zh, PLANES, 1)).astype(BF16)
    zf[PLANES : 2 * PLANES, :] = (z - zh).astype(BF16)
    h, l = split(x_matrix(k[5:6]))
    x1f[0:WIDTH, :] = h
    x1f[WIDTH : 2 * WIDTH, :] = h
    x2f[...] = l

    def hot(rows, offset):
        i = lax.broadcasted_iota(jnp.int32, (rows, WIDTH), 0)
        j = lax.broadcasted_iota(jnp.int32, (rows, WIDTH), 1)
        return jnp.where(j - i == offset, 1.0, 0.0)

    yd[...] = jnp.where(valid, hot(ROWS, shifts[0, 1] + ROWS), 0.0).astype(BF16)
    xd[...] = hot(WIDTH, -shifts[0, 2]).astype(BF16)


def all_mats_kernel(t0, t1, t2, t3, coverage, zb, x1b, x2b):
    v = lax.axis_index("view")
    block = strip_index() * ROWS // BLOCK
    for i, taps in enumerate((t0, t1, t2, t3)):
        k = normed(taps[...])
        zh, zl = split(toeplitz(k[3:4], PLANES, WIDTH - HALF))
        zb[i, 0:PLANES, :] = zh
        zb[i, PLANES : 2 * PLANES, :] = zl
        weight = coverage[lax.rem(v - i + VIEWS, VIEWS), block, 0].astype(F32)
        h, l = split(weight * x_matrix(k[2:3]))
        at = slice(i * WIDTH, (i + 1) * WIDTH)
        x1b[at, :] = h
        x1b[VIEWS * WIDTH + i * WIDTH : VIEWS * WIDTH + (i + 1) * WIDTH, :] = h
        x2b[at, :] = l


def y_stage(pair, matrix, put):
    loop(PLANES // 2, lambda c: put(2 * c, dot(matrix, pair(2 * c))))


def filtered_rows(t):
    def put(p, o):
        o = o[0:ROWS] + o[ROWS : 2 * ROWS]
        t[pl.ds(p * ROWS, ROWS), :] = o[:, 0:WIDTH]
        t[pl.ds(p * ROWS + ROWS, ROWS), :] = o[:, WIDTH : 2 * WIDTH]

    return put


def z_stage(t, u, zf):
    def body(c):
        first, second = (pl.ds(2 * c + k, PLANES, stride=ROWS) for k in (0, 1))
        h0, l0 = split(t[first, :])
        h1, l1 = split(t[second, :])
        rhs = jnp.concatenate(
            [jnp.concatenate([h0, h1], axis=1), jnp.concatenate([l0, l1], axis=1)], axis=0
        )
        o = dot(zf, rhs)
        o = o[0:PLANES] + o[PLANES : 2 * PLANES]
        u[first, :] = o[:, 0:WIDTH]
        u[second, :] = o[:, WIDTH : 2 * WIDTH]

    loop(ROWS // 2, body)


def x_stage(t, x1, x2, emit):
    def body(c):
        h, l = split(t[pl.ds(c * CHUNK, CHUNK), :])
        emit(c, dot(jnp.concatenate([h, l], axis=1), x1) + dot(h, x2))

    loop(FLAT // CHUNK, body)


def gather_first(f, slab, other, far_a, far_b):
    g = lax.axis_index("gz")
    low, high = slice(0, PLANES // 2), slice(PLANES // 2, PLANES)

    @pl.when(g == 0)
    def _():
        f[low, ROWS:SPAN, :] = slab[...]
        f[high, ROWS:SPAN, :] = other[...]
        f[low, 0:ROWS, :] = far_a[...]
        f[high, 0:ROWS, :] = far_b[...]

    @pl.when(g == 1)
    def _():
        f[high, 0 : 2 * ROWS, :] = slab[...]
        f[low, 0 : 2 * ROWS, :] = other[...]
        f[high, 2 * ROWS : SPAN, :] = far_a[...]
        f[low, 2 * ROWS : SPAN, :] = far_b[...]


def window_pair(f):
    return lambda p: jnp.concatenate([f[p], f[p + 1]], axis=1)


def strips_pair(far, own, near):
    def pair(p):
        sides = [jnp.concatenate([ref[p], ref[p + 1]], axis=1) for ref in (far, own, near)]
        return jnp.concatenate(sides, axis=0)

    return pair


def chunk_planes(c):
    return pl.ds(c * (CHUNK // ROWS), CHUNK // ROWS)


def as_planes(x):
    return x.reshape(CHUNK // ROWS, ROWS, WIDTH)


def first_pred_kernel(slab, other, far_a, far_b, yw, zf, x1, x2, pred, f, t, u):
    gather_first(f, slab, other, far_a, far_b)
    y_stage(window_pair(f), yw[:, 0:SPAN], filtered_rows(t))
    z_stage(t, u, zf[...])

    def emit(c, x):
        pred[pl.ds(c * CHUNK, CHUNK), :] = x

    x_stage(u, x1[...], x2[...], emit)


def first_ratio_kernel(slab, other, far_a, far_b, yd, xd, shifts, pred, data, ratio, f, d):
    gather_first(f, slab, other, far_a, far_b)
    d[SHIFT : SHIFT + PLANES] = jnp.zeros((PLANES, ROWS, WIDTH), BF16)
    up = SHIFT - shifts[0, 0]

    def put(p, o):
        o = o.astype(BF16)
        d[p + up] = o[:, 0:WIDTH]
        d[p + 1 + up] = o[:, WIDTH : 2 * WIDTH]

    y_stage(window_pair(f), yd[:, 0:SPAN], put)

    def body(c):
        moved = d[pl.ds(SHIFT + c * (CHUNK // ROWS), CHUNK // ROWS)]
        got = dot(moved.reshape(CHUNK, WIDTH), xd[...])
        data[chunk_planes(c)] = as_planes(got).astype(BF16)
        quot = got / (pred[pl.ds(c * CHUNK, CHUNK), :] + 0.05)
        ratio[chunk_planes(c)] = as_planes(quot).astype(BF16)

    loop(FLAT // CHUNK, body)


def back_y_kernel(far, own, near, yb, _, o0, o1, o2, o3, t):
    y_stage(strips_pair(far, own, near), yb[:, 0:SPAN], filtered_rows(t))
    v = lax.axis_index("view")
    for i, out in enumerate((o0, o1, o2, o3)):
        q = lax.rem(v + i, VIEWS) * QUARTER
        for r in range(QUARTER):
            out[r * PLANES : (r + 1) * PLANES, :] = t[
                pl.ds(q + r, PLANES, stride=ROWS), :
            ].astype(BF16)


def compose_kernel(p0, p1, p2, p3, own, c):
    v = lax.axis_index("view")
    for j, ref in enumerate((p0, p1, p2, p3)):
        q = pl.multiple_of(lax.rem(v - j + VIEWS, VIEWS) * QUARTER, QUARTER)
        c[:, pl.ds(q, QUARTER), :] = ref[...].astype(F32)
    own[...] = c[...].astype(BF16)


def next_ratio_kernel(far, own, near, yf, zf, x1, x2, data, ratio, t, u):
    y_stage(strips_pair(far, own, near), yf[:, 0:SPAN], filtered_rows(t))
    z_stage(t, u, zf[...])

    def emit(c, x):
        quot = as_planes(x + 0.05)
        ratio[chunk_planes(c)] = (data[chunk_planes(c)].astype(F32) / quot).astype(BF16)

    x_stage(u, x1[...], x2[...], emit)


def view_count(coverage):
    block = strip_index() * ROWS // BLOCK
    count = coverage[0, block, 0]
    for w in range(1, VIEWS):
        count = count + coverage[w, block, 0]
    return count.astype(F32)


def weighted_total(terms, zb, x1b, x2b, hl):
    both = VIEWS * WIDTH
    for i, term in enumerate(terms):
        zmat = zb[i, :, 0:PLANES]
        high, low = slice(i * WIDTH, (i + 1) * WIDTH), slice(both + i * WIDTH, both + (i + 1) * WIDTH)
        for u in range(QUARTER // 2):
            at = 2 * u * PLANES
            rhs = jnp.concatenate(
                [term[at : at + PLANES, :], term[at + PLANES : at + 2 * PLANES, :]], axis=1
            )
            o = dot(zmat, rhs)
            zh, zl = split(o[0:PLANES] + o[PLANES : 2 * PLANES])
            hl[at : at + PLANES, high] = zh[:, 0:WIDTH]
            hl[at : at + PLANES, low] = zl[:, 0:WIDTH]
            at = at + PLANES
            hl[at : at + PLANES, high] = zh[:, WIDTH : 2 * WIDTH]
            hl[at : at + PLANES, low] = zl[:, WIDTH : 2 * WIDTH]
    return dot(hl[...], x1b[...]) + dot(hl[:, 0:both], x2b[...])


def updated(old, acc, count, new):
    for r in range(QUARTER):
        at = pl.ds(r, PLANES, stride=QUARTER)
        new[at, :] = old[at, :] * acc[r * PLANES : (r + 1) * PLANES, :] / count


def first_update_kernel(
    t0, t1, t2, t3, coverage, mine, theirs, zb, x1b, x2b, field, sent, hl, fq
):
    g = lax.axis_index("gz")
    half = QFLAT // 2

    @pl.when(g == 0)
    def _():
        fq[0:half, :] = mine[...]
        fq[half:QFLAT, :] = theirs[...]

    @pl.when(g == 1)
    def _():
        fq[half:QFLAT, :] = mine[...]
        fq[0:half, :] = theirs[...]

    acc = weighted_total((t0, t1, t2, t3), zb, x1b, x2b, hl)
    updated(fq, acc, view_count(coverage), field)
    sent[...] = field[...].reshape(PLANES, QUARTER, WIDTH).astype(BF16)


def as_rows(x):
    return x[...].astype(F32).reshape(QFLAT, WIDTH)


def last_update_kernel(t0, t1, t2, t3, coverage, old, sent, zb, x1b, x2b, coded, hl, new):
    acc = weighted_total((t0, t1, t2, t3), zb, x1b, x2b, hl)
    updated(old, acc, view_count(coverage), new)
    known = as_rows(sent)

    def total(x):
        return jnp.sum(jnp.sum(x, axis=0, keepdims=True), axis=1, keepdims=True)

    scale = total(new[...] * known) / jnp.maximum(total(known * known), 1e-30)
    scale = scale.astype(BF16).astype(F32)
    coded[0:QFLAT, :] = new[...] - scale * known
    coded[QFLAT : QFLAT + TAIL, :] = jnp.broadcast_to(scale, (TAIL, WIDTH))


def decoded(coded, known, at, lines):
    scale = coded[QFLAT : QFLAT + 1, :]
    value = known[at].astype(F32)
    return coded[lines, :].reshape(value.shape) + scale.reshape(1, 1, WIDTH) * value


def halves_kernel(p0, p1, p2, p3, s0, s1, s2, s3, give):
    g = lax.axis_index("gz")
    half = PLANES // 2
    at = pl.ds((1 - g) * half, half)
    lines = pl.ds(pl.multiple_of((1 - g) * half * QUARTER, half * QUARTER), half * QUARTER)
    for j, (ref, sent) in enumerate(((p0, s0), (p1, s1), (p2, s2), (p3, s3))):
        give[j] = decoded(ref, sent, at, lines)


def final_kernel(p0, p1, p2, p3, s0, s1, s2, s3, got, out):
    v, g = lax.axis_index("view"), lax.axis_index("gz")
    half = PLANES // 2
    at = pl.ds(g * half, half)
    lines = pl.ds(pl.multiple_of(g * half * QUARTER, half * QUARTER), half * QUARTER)
    for j, (ref, sent) in enumerate(((p0, s0), (p1, s1), (p2, s2), (p3, s3))):
        q = lax.rem(v - j + VIEWS, VIEWS) * QUARTER
        here = pl.multiple_of(g * ROWS + q, QUARTER)
        there = pl.multiple_of((1 - g) * ROWS + q, QUARTER)
        out[:, pl.ds(here, QUARTER), :] = decoded(ref, sent, at, lines)
        out[:, pl.ds(there, QUARTER), :] = got[j]


def steps(count, shift):
    return [(i, (i + shift) % count) for i in range(count)]


def on_device(estimate, views, shifts, kernels, coverage):
    strips = lax.axis_size("xy")
    count = 2 * strips
    half = PLANES // 2
    quart = (QFLAT, WIDTH)
    strip = arr((PLANES, ROWS, WIDTH), BF16)
    both = [kernels[0], kernels[0][:, ::-1]]
    taps = jnp.pad(jnp.concatenate(both, axis=0), ((0, 2), (0, WIDTH - kernels.shape[2])))

    piece = arr((half, ROWS, WIDTH), BF16)
    eighth = arr((half, QUARTER, WIDTH), F32)
    eb, em, eo, mine, theirs = call(
        prep_estimate_kernel,
        [arr((half, 2 * ROWS, WIDTH), BF16), piece, piece, eighth, eighth],
    )(estimate)
    vm, vo = call(prep_views_kernel, [piece, piece])(views)

    outward, inward = [], []
    for s in range(strips):
        outward += [(2 * s, 2 * ((s + 1) % strips)), (2 * s + 1, 2 * ((s - 1) % strips) + 1)]
        inward += [(2 * s, 2 * ((s - 1) % strips) + 1), (2 * s + 1, 2 * ((s + 1) % strips))]
    swap = steps(2, 1)
    e_far = [lax.ppermute(eo, STRIPS, outward), lax.ppermute(em, STRIPS, inward)]
    e_all = [eb, lax.ppermute(eb, "gz", swap)] + e_far
    v_far = [lax.ppermute(vo, STRIPS, outward), lax.ppermute(vm, STRIPS, inward)]
    v_all = [views[0], lax.ppermute(views[0], "gz", swap)] + v_far

    yw, yf, yb, zf, x1f, x2f, yd, xd = call(
        own_mats_kernel,
        [
            arr((2 * ROWS, WIDTH), BF16),
            arr((2 * ROWS, WIDTH), BF16),
            arr((2 * ROWS, WIDTH), BF16),
            arr((2 * PLANES, WIDTH), BF16),
            arr((2 * WIDTH, WIDTH), BF16),
            arr((WIDTH, WIDTH), BF16),
            arr((ROWS, WIDTH), BF16),
            arr((WIDTH, WIDTH), BF16),
        ],
        smem=(1,),
    )(taps, shifts)

    window = pltpu.VMEM((PLANES, SPAN, WIDTH), BF16)
    shifted = pltpu.VMEM((PLANES + 2 * SHIFT, ROWS, WIDTH), BF16)
    flat = pltpu.VMEM((FLAT, WIDTH), F32)
    cube = pltpu.VMEM((PLANES, ROWS, WIDTH), F32)
    pairs = pltpu.VMEM((QFLAT, 2 * VIEWS * WIDTH), BF16)
    total = pltpu.VMEM(quart, F32)

    pred = call(first_pred_kernel, arr((FLAT, WIDTH), F32), [window, flat, flat])(
        *e_all, yw, zf, x1f, x2f
    )
    data, ratio = call(first_ratio_kernel, [strip, strip], [window, shifted], smem=(6,))(
        *v_all, yd, xd, shifts, pred
    )

    across = [(i, (i + 1 if i % 2 else i - 1) % count) for i in range(count)]

    def neighbours(x):
        return lax.ppermute(x, STRIPS, across), lax.ppermute(x, "gz", swap)

    def from_views(x):
        return [x] + [lax.ppermute(x, "view", steps(VIEWS, i)) for i in range(1, VIEWS)]

    late, theirs, _ = lax.optimization_barrier((taps, theirs, ratio))
    theirs = lax.ppermute(theirs, "gz", swap)
    zb, x1b, x2b = call(
        all_mats_kernel,
        [
            arr((VIEWS, 2 * PLANES, WIDTH), BF16),
            arr((2 * VIEWS * WIDTH, WIDTH), BF16),
            arr((VIEWS * WIDTH, WIDTH), BF16),
        ],
        smem=(4,),
    )(*from_views(late), coverage)

    field = None
    for step in range(ITERS):
        far, near = neighbours(ratio)
        parts = call(back_y_kernel, [arr(quart, BF16)] * VIEWS, [flat])(far, ratio, near, yb, zb)
        terms = [parts[0]] + [
            lax.ppermute(parts[i], "view", steps(VIEWS, i)) for i in range(1, VIEWS)
        ]
        if step == 0:
            field, sent = call(
                first_update_kernel,
                [arr(quart, F32), arr((PLANES, QUARTER, WIDTH), BF16)],
                [pairs, total],
                smem=(4,),
            )(
                *terms,
                coverage,
                mine.reshape(QFLAT // 2, WIDTH),
                theirs.reshape(QFLAT // 2, WIDTH),
                zb,
                x1b,
                x2b,
            )
            beyond = lax.ppermute(sent, STRIPS, across)
            sent = from_views(sent)
            outer = from_views(beyond)
            own = call(compose_kernel, strip, [cube])(*sent)
            near = lax.ppermute(own, "gz", swap)
            far = call(compose_kernel, strip, [cube])(*outer)
            ratio = call(next_ratio_kernel, strip, [flat, flat])(
                far, own, near, yf, zf, x1f, x2f, data
            )
        else:
            coded = call(
                last_update_kernel,
                arr((QFLAT + TAIL, WIDTH), F32),
                [pairs, total],
                smem=(4,),
            )(*terms, coverage, field, sent[0], zb, x1b, x2b)
    coded = lax.optimization_barrier(coded.astype(F16))
    pieces = [lax.optimization_barrier(x).astype(F32) for x in from_views(coded)]
    give = call(halves_kernel, arr((VIEWS, half, QUARTER, WIDTH), F32))(*pieces, *sent)
    got = lax.ppermute(give, "gz", swap)
    return call(final_kernel, arr((half, 2 * ROWS, WIDTH), F32))(*pieces, *sent, got)


def solution(mesh):
    placed = (
        P("gz", "xy", None),
        P("view", "gz", "xy", None),
        P("view", None),
        P("view", None, None),
        P(),
    )
    return jax.shard_map(
        on_device, mesh=mesh, in_specs=placed, out_specs=P("gz", "xy", None), check_vma=False
    )
```

profile of v0, /device:TPU:0, one launch (start us, length us, event | category | flops | bytes accessed | tf_op | source)
XLA Modules:
  0.0 118.7 jit_solution(10227974554686169318)
XLA Ops:
  2.1 1.7 %collective-permute-start.4 = (bf16[32,32,128]{2,1,0:T(8,128)(2,1)S(1)}, bf16[32,32,128]{2,1,0:T(8,128)(2,1)S(1)}, u32[]{:S(2)}, u32[]{:S(2)}) collective-permute-start(bf16[32,32,128]{2,1,0:T(8,128)(2,1)S(1)} %get-tuple-element.42), channel_id=1, source_target_pairs={{0,2},{1,31},{2,4},{3,1},{4,6},{5,3},{6,8},{7,5},{8,10},{9,7},{10,... | collective-permute-start | bytes 786440 | tf_op jit(solution)/shard_map/ppermute | solution.py:446
  3.8 5.1 %collective-permute-start = (bf16[32,64,128]{2,1,0:T(8,128)(2,1)S(1)}, bf16[32,64,128]{2,1,0:T(8,128)(2,1)S(1)}, u32[]{:S(2)}, u32[]{:S(2)}) collective-permute-start(bf16[32,64,128]{2,1,0:T(8,128)(2,1)S(1)} %bitcast.6), channel_id=1, source_target_pairs={{0,1},{1,0},{2,3},{3,2},{4,5},{5,4},{6,7},{7,6},{8,9},{9,8},{10,11... | collective-permute-start | bytes 1572872 | tf_op jit(solution)/shard_map/ppermute | solution.py:449
  11.5 1.6 %collective-permute-done.4.far_a = bf16[32,32,128]{2,1,0:T(8,128)(2,1)S(1)} collective-permute-done((bf16[32,32,128]{2,1,0:T(8,128)(2,1)S(1)}, bf16[32,32,128]{2,1,0:T(8,128)(2,1)S(1)}, u32[]{:S(2)}, u32[]{:S(2)}) %collective-permute-start.4) | collective-permute-done | bytes 262176 | tf_op jit(solution)/shard_map/ppermute | solution.py:446
  13.1 5.9 %collective-permute-start.2 = (bf16[32,32,128]{2,1,0:T(8,128)(2,1)}, bf16[32,32,128]{2,1,0:T(8,128)(2,1)S(1)}, u32[]{:S(2)}, u32[]{:S(2)}) collective-permute-start(bf16[32,32,128]{2,1,0:T(8,128)(2,1)} %get-tuple-element.38), channel_id=1, source_target_pairs={{0,31},{1,2},{2,1},{3,4},{4,3},{5,6},{6,5},{7,8},{8,7},{9,10},{10,... | collective-permute-start | bytes 786440 | tf_op jit(solution)/shard_map/ppermute | solution.py:448
  20.5 2.3 %shard_map.58.pred = f32[2048,128]{1,0:T(8,128)S(1)} custom-call(bf16[32,64,128]{2,1,0:T(8,128)(2,1)S(1)} %get-tuple-element.41.slab, bf16[32,64,128]{2,1,0:T(8,128)(2,1)S(1)} %collective-permute-done.3.other, bf16[32,32,128]{2,1,0:T(8,128)(2,1)S(1)} %collective-permute-done.4.far_a, bf16[32,32,128]{2,1,0:T(8,128)(2,1)S(1)} %collective-permute-done.5.far_b, ...), custom_call_target="tpu_custom_call" | custom-call | flops 100000000 | bytes 4194304 | tf_op jit(solution)/shard_map/pallas_call | solution.py:46
  25.2 4.4 %collective-permute-start.6 = (bf16[64,32,128]{2,1,0:T(8,128)(2,1)S(1)}, bf16[64,32,128]{2,1,0:T(8,128)(2,1)S(1)}, u32[]{:S(2)}, u32[]{:S(2)}) collective-permute-start(bf16[64,32,128]{2,1,0:T(8,128)(2,1)S(1)} %get-tuple-element.48.own), channel_id=1, source_target_pairs={{0,31},{1,2},{2,1},{3,4},{4,3},{5,6},{6,5},{7,8},{8,7},{9,10},{10,... | collective-permute-start | bytes 1572872 | tf_op jit(solution)/shard_map/ppermute | solution.py:483
  29.7 2.8 %collective-permute-start.10 = (f32[8,128]{1,0:T(8,128)S(1)}, f32[8,128]{1,0:T(8,128)S(1)}, u32[]{:S(2)}, u32[]{:S(2)}) collective-permute-start(f32[8,128]{1,0:T(8,128)S(1)} %select_maximum_fusion.taps.t0), channel_id=1, source_target_pairs={{0,96},{32,0},{64,32},{96,64},{1,97},{33,1},{65,33},{97,65},{2,98}... | collective-permute-start | bytes 12296 | tf_op jit(solution)/shard_map/ppermute | solution.py:486
  32.4 2.3 %collective-permute-start.9 = (f32[8,128]{1,0:T(8,128)S(1)}, f32[8,128]{1,0:T(8,128)S(1)}, u32[]{:S(2)}, u32[]{:S(2)}) collective-permute-start(f32[8,128]{1,0:T(8,128)S(1)} %select_maximum_fusion.taps.t0), channel_id=1, source_target_pairs={{0,64},{32,96},{64,0},{96,32},{1,65},{33,97},{65,1},{97,33},{2,66}... | collective-permute-start | bytes 12296 | tf_op jit(solution)/shard_map/ppermute | solution.py:486
  34.9 2.3 %collective-permute-done.8.t1 = f32[8,128]{1,0:T(8,128)S(1)} collective-permute-done((f32[8,128]{1,0:T(8,128)S(1)}, f32[8,128]{1,0:T(8,128)S(1)}, u32[]{:S(2)}, u32[]{:S(2)}) %collective-permute-start.8) | collective-permute-done | bytes 4128 | tf_op jit(solution)/shard_map/ppermute | solution.py:486
  40.5 3.9 %collective-permute-start.12 = (bf16[512,128]{1,0:T(8,128)(2,1)S(1)}, bf16[512,128]{1,0:T(8,128)(2,1)S(1)}, u32[]{:S(2)}, u32[]{:S(2)}) collective-permute-start(bf16[512,128]{1,0:T(8,128)(2,1)S(1)} %get-tuple-element.55), channel_id=1, source_target_pairs={{0,64},{32,96},{64,0},{96,32},{1,65},{33,97},{65,1},{97,33},{2,66}... | collective-permute-start | bytes 393224 | tf_op jit(solution)/shard_map/ppermute | solution.py:505
  44.6 2.1 %collective-permute-done.11.t1 = bf16[512,128]{1,0:T(8,128)(2,1)S(1)} collective-permute-done((bf16[512,128]{1,0:T(8,128)(2,1)S(1)}, bf16[512,128]{1,0:T(8,128)(2,1)S(1)}, u32[]{:S(2)}, u32[]{:S(2)}) %collective-permute-start.11) | collective-permute-done | bytes 131104 | tf_op jit(solution)/shard_map/ppermute | solution.py:505
  46.8 2.9 %collective-permute-done.12.t2 = bf16[512,128]{1,0:T(8,128)(2,1)S(1)} collective-permute-done((bf16[512,128]{1,0:T(8,128)(2,1)S(1)}, bf16[512,128]{1,0:T(8,128)(2,1)S(1)}, u32[]{:S(2)}, u32[]{:S(2)}) %collective-permute-start.12) | collective-permute-done | bytes 131104 | tf_op jit(solution)/shard_map/ppermute | solution.py:505
  49.7 1.8 %shard_map.62 = (f32[512,128]{1,0:T(8,128)S(1)}, bf16[64,8,128]{2,1,0:T(8,128)(2,1)S(1)}) custom-call(bf16[512,128]{1,0:T(8,128)(2,1)S(1)} %get-tuple-element.53.t0, bf16[512,128]{1,0:T(8,128)(2,1)S(1)} %collective-permute-done.11.t1, bf16[512,128]{1,0:T(8,128)(2,1)S(1)} %collective-permute-done.12.t2, bf16[512,128]{1,0:T(8,128)(2,1)S(1)} %collective-permute-done.13.t3, ...), custom_call_target="tpu_custom_call" | custom-call | flops 100000000 | bytes 4194304 | tf_op jit(solution)/shard_map/pallas_call | solution.py:46
  52.3 2.8 %collective-permute-start.20 = (bf16[64,8,128]{2,1,0:T(8,128)(2,1)S(1)}, bf16[64,8,128]{2,1,0:T(8,128)(2,1)S(1)}, u32[]{:S(2)}, u32[]{:S(2)}) collective-permute-start(bf16[64,8,128]{2,1,0:T(8,128)(2,1)S(1)} %get-tuple-element.61.p0.sent.s0), channel_id=1, source_target_pairs={{0,64},{32,96},{64,0},{96,32},{1,65},{33,97},{65,1},{97,33},{2,66}... | collective-permute-start | bytes 393224 | tf_op jit(solution)/shard_map/ppermute | solution.py:486
  55.5 3.4 %collective-permute-done.19.p1.s1 = bf16[64,8,128]{2,1,0:T(8,128)(2,1)S(1)} collective-permute-done((bf16[64,8,128]{2,1,0:T(8,128)(2,1)S(1)}, bf16[64,8,128]{2,1,0:T(8,128)(2,1)S(1)}, u32[]{:S(2)}, u32[]{:S(2)}) %collective-permute-start.19) | collective-permute-done | bytes 131104 | tf_op jit(solution)/shard_map/ppermute | solution.py:486
  60.7 4.1 %collective-permute-start.15 = (bf16[64,8,128]{2,1,0:T(8,128)(2,1)S(1)}, bf16[64,8,128]{2,1,0:T(8,128)(2,1)S(1)}, u32[]{:S(2)}, u32[]{:S(2)}) collective-permute-start(bf16[64,8,128]{2,1,0:T(8,128)(2,1)S(1)} %get-tuple-element.61.p0.sent.s0), channel_id=1, source_target_pairs={{0,31},{1,2},{2,1},{3,4},{4,3},{5,6},{6,5},{7,8},{8,7},{9,10},{10,... | collective-permute-start | bytes 393224 | tf_op jit(solution)/shard_map/ppermute | solution.py:522
  64.7 3.9 %collective-permute-done.15.p0 = bf16[64,8,128]{2,1,0:T(8,128)(2,1)S(1)} collective-permute-done((bf16[64,8,128]{2,1,0:T(8,128)(2,1)S(1)}, bf16[64,8,128]{2,1,0:T(8,128)(2,1)S(1)}, u32[]{:S(2)}, u32[]{:S(2)}) %collective-permute-start.15) | collective-permute-done | bytes 131104 | tf_op jit(solution)/shard_map/ppermute | solution.py:522
  69.5 3.2 %collective-permute-start.17 = (bf16[64,8,128]{2,1,0:T(8,128)(2,1)S(1)}, bf16[64,8,128]{2,1,0:T(8,128)(2,1)S(1)}, u32[]{:S(2)}, u32[]{:S(2)}) collective-permute-start(bf16[64,8,128]{2,1,0:T(8,128)(2,1)S(1)} %collective-permute-done.15.p0), channel_id=1, source_target_pairs={{0,64},{32,96},{64,0},{96,32},{1,65},{33,97},{65,1},{97,33},{2,66}... | collective-permute-start | bytes 393224 | tf_op jit(solution)/shard_map/ppermute | solution.py:486
  72.8 2.1 %collective-permute-done.16.p1 = bf16[64,8,128]{2,1,0:T(8,128)(2,1)S(1)} collective-permute-done((bf16[64,8,128]{2,1,0:T(8,128)(2,1)S(1)}, bf16[64,8,128]{2,1,0:T(8,128)(2,1)S(1)}, u32[]{:S(2)}, u32[]{:S(2)}) %collective-permute-start.16) | collective-permute-done | bytes 131104 | tf_op jit(solution)/shard_map/ppermute | solution.py:486
  74.8 2.2 %collective-permute-done.17.p2 = bf16[64,8,128]{2,1,0:T(8,128)(2,1)S(1)} collective-permute-done((bf16[64,8,128]{2,1,0:T(8,128)(2,1)S(1)}, bf16[64,8,128]{2,1,0:T(8,128)(2,1)S(1)}, u32[]{:S(2)}, u32[]{:S(2)}) %collective-permute-start.17) | collective-permute-done | bytes 131104 | tf_op jit(solution)/shard_map/ppermute | solution.py:486
  77.9 2.2 %shard_map.65.own = bf16[64,32,128]{2,1,0:T(8,128)(2,1)S(1)} custom-call(bf16[64,32,128]{2,1,0:T(8,128)(2,1)S(1)} %shard_map.63.far, bf16[64,32,128]{2,1,0:T(8,128)(2,1)S(1)} %shard_map.64.own, bf16[64,32,128]{2,1,0:T(8,128)(2,1)S(1)} %collective-permute-done.22.near, bf16[64,128]{1,0:T(8,128)(2,1)S(1)} %get-tuple-element.62.yf, ...), custom_call_target="tpu_custom_call" | custom-call | flops 100000000 | bytes 4194304 | tf_op jit(solution)/shard_map/pallas_call | solution.py:46
  80.1 3.0 %collective-permute-start.23 = (bf16[64,32,128]{2,1,0:T(8,128)(2,1)S(1)}, bf16[64,32,128]{2,1,0:T(8,128)(2,1)S(1)}, u32[]{:S(2)}, u32[]{:S(2)}) collective-permute-start(bf16[64,32,128]{2,1,0:T(8,128)(2,1)S(1)} %shard_map.65.own), channel_id=1, source_target_pairs={{0,31},{1,2},{2,1},{3,4},{4,3},{5,6},{6,5},{7,8},{8,7},{9,10},{10,... | collective-permute-start | bytes 1572872 | tf_op jit(solution)/shard_map/ppermute | solution.py:483
  83.1 9.0 %collective-permute-done.23.far = bf16[64,32,128]{2,1,0:T(8,128)(2,1)S(1)} collective-permute-done((bf16[64,32,128]{2,1,0:T(8,128)(2,1)S(1)}, bf16[64,32,128]{2,1,0:T(8,128)(2,1)S(1)}, u32[]{:S(2)}, u32[]{:S(2)}) %collective-permute-start.23) | collective-permute-done | bytes 524320 | tf_op jit(solution)/shard_map/ppermute | solution.py:483
  93.5 3.2 %collective-permute-start.26 = (bf16[512,128]{1,0:T(8,128)(2,1)S(1)}, bf16[512,128]{1,0:T(8,128)(2,1)S(1)}, u32[]{:S(2)}, u32[]{:S(2)}) collective-permute-start(bf16[512,128]{1,0:T(8,128)(2,1)S(1)} %get-tuple-element.66), channel_id=1, source_target_pairs={{0,64},{32,96},{64,0},{96,32},{1,65},{33,97},{65,1},{97,33},{2,66}... | collective-permute-start | bytes 393224 | tf_op jit(solution)/shard_map/ppermute | solution.py:505
  97.3 2.3 %collective-permute-done.25.t1 = bf16[512,128]{1,0:T(8,128)(2,1)S(1)} collective-permute-done((bf16[512,128]{1,0:T(8,128)(2,1)S(1)}, bf16[512,128]{1,0:T(8,128)(2,1)S(1)}, u32[]{:S(2)}, u32[]{:S(2)}) %collective-permute-start.25) | collective-permute-done | bytes 131104 | tf_op jit(solution)/shard_map/ppermute | solution.py:505
  99.6 2.7 %collective-permute-done.26.t2 = bf16[512,128]{1,0:T(8,128)(2,1)S(1)} collective-permute-done((bf16[512,128]{1,0:T(8,128)(2,1)S(1)}, bf16[512,128]{1,0:T(8,128)(2,1)S(1)}, u32[]{:S(2)}, u32[]{:S(2)}) %collective-permute-start.26) | collective-permute-done | bytes 131104 | tf_op jit(solution)/shard_map/ppermute | solution.py:505
  103.5 1.9 %shard_map.67 = f32[520,128]{1,0:T(8,128)S(1)} custom-call(bf16[512,128]{1,0:T(8,128)(2,1)S(1)} %get-tuple-element.64.t0, bf16[512,128]{1,0:T(8,128)(2,1)S(1)} %collective-permute-done.25.t1, bf16[512,128]{1,0:T(8,128)(2,1)S(1)} %collective-permute-done.26.t2, bf16[512,128]{1,0:T(8,128)(2,1)S(1)} %collective-permute-done.27.t3, ...), custom_call_target="tpu_custom_call" | custom-call | flops 100000000 | bytes 4194304 | tf_op jit(solution)/shard_map/pallas_call | solution.py:46
  105.5 1.8 %collective-permute-start.28 = (f16[520,128]{1,0:T(8,128)(2,1)S(1)}, f16[520,128]{1,0:T(8,128)(2,1)S(1)}, u32[]{:S(2)}, u32[]{:S(2)}) collective-permute-start(f16[520,128]{1,0:T(8,128)(2,1)S(1)} %convert_element_type.17), channel_id=1, source_target_pairs={{0,32},{32,64},{64,96},{96,0},{1,33},{33,65},{65,97},{97,1},{2,34}... | collective-permute-start | bytes 399368 | tf_op jit(solution)/shard_map/ppermute | solution.py:486
  107.3 3.2 %collective-permute-start.29 = (f16[520,128]{1,0:T(8,128)(2,1)S(1)}, f16[520,128]{1,0:T(8,128)(2,1)S(1)}, u32[]{:S(2)}, u32[]{:S(2)}) collective-permute-start(f16[520,128]{1,0:T(8,128)(2,1)S(1)} %convert_element_type.17), channel_id=1, source_target_pairs={{0,64},{32,96},{64,0},{96,32},{1,65},{33,97},{65,1},{97,33},{2,66}... | collective-permute-start | bytes 399368 | tf_op jit(solution)/shard_map/ppermute | solution.py:486
  110.5 1.5 %collective-permute-done.28 = f16[520,128]{1,0:T(8,128)(2,1)S(1)} collective-permute-done((f16[520,128]{1,0:T(8,128)(2,1)S(1)}, f16[520,128]{1,0:T(8,128)(2,1)S(1)}, u32[]{:S(2)}, u32[]{:S(2)}) %collective-permute-start.28) | collective-permute-done | bytes 133152 | tf_op jit(solution)/shard_map/ppermute | solution.py:486
  112.0 2.9 %collective-permute-done.29 = f16[520,128]{1,0:T(8,128)(2,1)S(1)} collective-permute-done((f16[520,128]{1,0:T(8,128)(2,1)S(1)}, f16[520,128]{1,0:T(8,128)(2,1)S(1)}, u32[]{:S(2)}, u32[]{:S(2)}) %collective-permute-start.29) | collective-permute-done | bytes 133152 | tf_op jit(solution)/shard_map/ppermute | solution.py:486
  115.7 1.9 %collective-permute-done.31.got = f32[4,32,8,128]{3,2,1,0:T(8,128)S(1)} collective-permute-done((f32[4,32,8,128]{3,2,1,0:T(8,128)S(1)}, f32[4,32,8,128]{3,2,1,0:T(8,128)S(1)}, u32[]{:S(2)}, u32[]{:S(2)}) %collective-permute-start.31) | collective-permute-done | bytes 524320 | tf_op jit(solution)/shard_map/ppermute | solution.py:541
  (70 shorter events, 22.2 us)
Async XLA Ops:
  2.1 18.4 %collective-permute-start.3 = (bf16[32,64,128]{2,1,0:T(8,128)(2,1)S(1)}, bf16[32,64,128]{2,1,0:T(8,128)(2,1)S(1)}, u32[]{:S(2)}, u32[]{:S(2)}) collective-permute-start(bf16[32,64,128]{2,1,0:T(8,128)(2,1)S(1)} %get-tuple-element.41.slab), channel_id=1, source_target_pairs={{0,1},{1,0},{2,3},{3,2},{4,5},{5,4},{6,7},{7,6},{8,9},{9,8},{10,11... | collective-permute-start | bytes 1572872 | tf_op jit(solution)/shard_map/ppermute | solution.py:447
  2.1 10.9 %collective-permute-start.4 = (bf16[32,32,128]{2,1,0:T(8,128)(2,1)S(1)}, bf16[32,32,128]{2,1,0:T(8,128)(2,1)S(1)}, u32[]{:S(2)}, u32[]{:S(2)}) collective-permute-start(bf16[32,32,128]{2,1,0:T(8,128)(2,1)S(1)} %get-tuple-element.42), channel_id=1, source_target_pairs={{0,2},{1,31},{2,4},{3,1},{4,6},{5,3},{6,8},{7,5},{8,10},{9,7},{10,... | collective-permute-start | bytes 786440 | tf_op jit(solution)/shard_map/ppermute | solution.py:446
  3.8 20.1 %collective-permute-start = (bf16[32,64,128]{2,1,0:T(8,128)(2,1)S(1)}, bf16[32,64,128]{2,1,0:T(8,128)(2,1)S(1)}, u32[]{:S(2)}, u32[]{:S(2)}) collective-permute-start(bf16[32,64,128]{2,1,0:T(8,128)(2,1)S(1)} %bitcast.6), channel_id=1, source_target_pairs={{0,1},{1,0},{2,3},{3,2},{4,5},{5,4},{6,7},{7,6},{8,9},{9,8},{10,11... | collective-permute-start | bytes 1572872 | tf_op jit(solution)/shard_map/ppermute | solution.py:449
  9.0 11.5 %collective-permute-start.5 = (bf16[32,32,128]{2,1,0:T(8,128)(2,1)}, bf16[32,32,128]{2,1,0:T(8,128)(2,1)S(1)}, u32[]{:S(2)}, u32[]{:S(2)}) collective-permute-start(bf16[32,32,128]{2,1,0:T(8,128)(2,1)} %get-tuple-element.43), channel_id=1, source_target_pairs={{0,31},{1,2},{2,1},{3,4},{4,3},{5,6},{6,5},{7,8},{8,7},{9,10},{10,... | collective-permute-start | bytes 786440 | tf_op jit(solution)/shard_map/ppermute | solution.py:446
  10.2 12.6 %collective-permute-start.1 = (bf16[32,32,128]{2,1,0:T(8,128)(2,1)}, bf16[32,32,128]{2,1,0:T(8,128)(2,1)S(1)}, u32[]{:S(2)}, u32[]{:S(2)}) collective-permute-start(bf16[32,32,128]{2,1,0:T(8,128)(2,1)} %get-tuple-element.37), channel_id=1, source_target_pairs={{0,2},{1,31},{2,4},{3,1},{4,6},{5,3},{6,8},{7,5},{8,10},{9,7},{10,... | collective-permute-start | bytes 786440 | tf_op jit(solution)/shard_map/ppermute | solution.py:448
  13.1 10.8 %collective-permute-start.2 = (bf16[32,32,128]{2,1,0:T(8,128)(2,1)}, bf16[32,32,128]{2,1,0:T(8,128)(2,1)S(1)}, u32[]{:S(2)}, u32[]{:S(2)}) collective-permute-start(bf16[32,32,128]{2,1,0:T(8,128)(2,1)} %get-tuple-element.38), channel_id=1, source_target_pairs={{0,31},{1,2},{2,1},{3,4},{4,3},{5,6},{6,5},{7,8},{8,7},{9,10},{10,... | collective-permute-start | bytes 786440 | tf_op jit(solution)/shard_map/ppermute | solution.py:448
  25.2 13.4 %collective-permute-start.6 = (bf16[64,32,128]{2,1,0:T(8,128)(2,1)S(1)}, bf16[64,32,128]{2,1,0:T(8,128)(2,1)S(1)}, u32[]{:S(2)}, u32[]{:S(2)}) collective-permute-start(bf16[64,32,128]{2,1,0:T(8,128)(2,1)S(1)} %get-tuple-element.48.own), channel_id=1, source_target_pairs={{0,31},{1,2},{2,1},{3,4},{4,3},{5,6},{6,5},{7,8},{8,7},{9,10},{10,... | collective-permute-start | bytes 1572872 | tf_op jit(solution)/shard_map/ppermute | solution.py:483
  29.7 9.0 %collective-permute-start.7 = (bf16[64,32,128]{2,1,0:T(8,128)(2,1)S(1)}, bf16[64,32,128]{2,1,0:T(8,128)(2,1)S(1)}, u32[]{:S(2)}, u32[]{:S(2)}) collective-permute-start(bf16[64,32,128]{2,1,0:T(8,128)(2,1)S(1)} %get-tuple-element.48.own), channel_id=1, source_target_pairs={{0,1},{1,0},{2,3},{3,2},{4,5},{5,4},{6,7},{7,6},{8,9},{9,8},{10,11... | collective-permute-start | bytes 1572872 | tf_op jit(solution)/shard_map/ppermute | solution.py:483
  29.7 5.2 %collective-permute-start.10 = (f32[8,128]{1,0:T(8,128)S(1)}, f32[8,128]{1,0:T(8,128)S(1)}, u32[]{:S(2)}, u32[]{:S(2)}) collective-permute-start(f32[8,128]{1,0:T(8,128)S(1)} %select_maximum_fusion.taps.t0), channel_id=1, source_target_pairs={{0,96},{32,0},{64,32},{96,64},{1,97},{33,1},{65,33},{97,65},{2,98}... | collective-permute-start | bytes 12296 | tf_op jit(solution)/shard_map/ppermute | solution.py:486
  32.4 4.8 %collective-permute-start.8 = (f32[8,128]{1,0:T(8,128)S(1)}, f32[8,128]{1,0:T(8,128)S(1)}, u32[]{:S(2)}, u32[]{:S(2)}) collective-permute-start(f32[8,128]{1,0:T(8,128)S(1)} %select_maximum_fusion.taps.t0), channel_id=1, source_target_pairs={{0,32},{32,64},{64,96},{96,0},{1,33},{33,65},{65,97},{97,1},{2,34}... | collective-permute-start | bytes 12296 | tf_op jit(solution)/shard_map/ppermute | solution.py:486
  32.4 5.1 %collective-permute-start.9 = (f32[8,128]{1,0:T(8,128)S(1)}, f32[8,128]{1,0:T(8,128)S(1)}, u32[]{:S(2)}, u32[]{:S(2)}) collective-permute-start(f32[8,128]{1,0:T(8,128)S(1)} %select_maximum_fusion.taps.t0), channel_id=1, source_target_pairs={{0,64},{32,96},{64,0},{96,32},{1,65},{33,97},{65,1},{97,33},{2,66}... | collective-permute-start | bytes 12296 | tf_op jit(solution)/shard_map/ppermute | solution.py:486
  34.8 9.8 %collective-permute-start.14 = (f32[32,8,128]{2,1,0:T(8,128)S(1)}, f32[32,8,128]{2,1,0:T(8,128)S(1)}, u32[]{:S(2)}, u32[]{:S(2)}) collective-permute-start(f32[32,8,128]{2,1,0:T(8,128)S(1)} %copy-done.4), channel_id=1, source_target_pairs={{0,1},{1,0},{2,3},{3,2},{4,5},{5,4},{6,7},{7,6},{8,9},{9,8},{10,11... | collective-permute-start | bytes 393224 | tf_op jit(solution)/shard_map/ppermute | solution.py:489
  39.6 7.1 %collective-permute-start.11 = (bf16[512,128]{1,0:T(8,128)(2,1)S(1)}, bf16[512,128]{1,0:T(8,128)(2,1)S(1)}, u32[]{:S(2)}, u32[]{:S(2)}) collective-permute-start(bf16[512,128]{1,0:T(8,128)(2,1)S(1)} %get-tuple-element.54), channel_id=1, source_target_pairs={{0,32},{32,64},{64,96},{96,0},{1,33},{33,65},{65,97},{97,1},{2,34}... | collective-permute-start | bytes 393224 | tf_op jit(solution)/shard_map/ppermute | solution.py:505
  40.5 9.2 %collective-permute-start.12 = (bf16[512,128]{1,0:T(8,128)(2,1)S(1)}, bf16[512,128]{1,0:T(8,128)(2,1)S(1)}, u32[]{:S(2)}, u32[]{:S(2)}) collective-permute-start(bf16[512,128]{1,0:T(8,128)(2,1)S(1)} %get-tuple-element.55), channel_id=1, source_target_pairs={{0,64},{32,96},{64,0},{96,32},{1,65},{33,97},{65,1},{97,33},{2,66}... | collective-permute-start | bytes 393224 | tf_op jit(solution)/shard_map/ppermute | solution.py:505
  44.4 5.3 %collective-permute-start.13 = (bf16[512,128]{1,0:T(8,128)(2,1)S(1)}, bf16[512,128]{1,0:T(8,128)(2,1)S(1)}, u32[]{:S(2)}, u32[]{:S(2)}) collective-permute-start(bf16[512,128]{1,0:T(8,128)(2,1)S(1)} %get-tuple-element.56), channel_id=1, source_target_pairs={{0,96},{32,0},{64,32},{96,64},{1,97},{33,1},{65,33},{97,65},{2,98}... | collective-permute-start | bytes 393224 | tf_op jit(solution)/shard_map/ppermute | solution.py:505
  51.4 7.5 %collective-permute-start.19 = (bf16[64,8,128]{2,1,0:T(8,128)(2,1)S(1)}, bf16[64,8,128]{2,1,0:T(8,128)(2,1)S(1)}, u32[]{:S(2)}, u32[]{:S(2)}) collective-permute-start(bf16[64,8,128]{2,1,0:T(8,128)(2,1)S(1)} %get-tuple-element.61.p0.sent.s0), channel_id=1, source_target_pairs={{0,32},{32,64},{64,96},{96,0},{1,33},{33,65},{65,97},{97,1},{2,34}... | collective-permute-start | bytes 393224 | tf_op jit(solution)/shard_map/ppermute | solution.py:486
  52.3 8.0 %collective-permute-start.20 = (bf16[64,8,128]{2,1,0:T(8,128)(2,1)S(1)}, bf16[64,8,128]{2,1,0:T(8,128)(2,1)S(1)}, u32[]{:S(2)}, u32[]{:S(2)}) collective-permute-start(bf16[64,8,128]{2,1,0:T(8,128)(2,1)S(1)} %get-tuple-element.61.p0.sent.s0), channel_id=1, source_target_pairs={{0,64},{32,96},{64,0},{96,32},{1,65},{33,97},{65,1},{97,33},{2,66}... | collective-permute-start | bytes 393224 | tf_op jit(solution)/shard_map/ppermute | solution.py:486
  55.1 5.2 %collective-permute-start.21 = (bf16[64,8,128]{2,1,0:T(8,128)(2,1)S(1)}, bf16[64,8,128]{2,1,0:T(8,128)(2,1)S(1)}, u32[]{:S(2)}, u32[]{:S(2)}) collective-permute-start(bf16[64,8,128]{2,1,0:T(8,128)(2,1)S(1)} %get-tuple-element.61.p0.sent.s0), channel_id=1, source_target_pairs={{0,96},{32,0},{64,32},{96,64},{1,97},{33,1},{65,33},{97,65},{2,98}... | collective-permute-start | bytes 393224 | tf_op jit(solution)/shard_map/ppermute | solution.py:486
  60.6 17.3 %collective-permute-start.22 = (bf16[64,32,128]{2,1,0:T(8,128)(2,1)S(1)}, bf16[64,32,128]{2,1,0:T(8,128)(2,1)S(1)}, u32[]{:S(2)}, u32[]{:S(2)}) collective-permute-start(bf16[64,32,128]{2,1,0:T(8,128)(2,1)S(1)} %shard_map.64.own), channel_id=1, source_target_pairs={{0,1},{1,0},{2,3},{3,2},{4,5},{5,4},{6,7},{7,6},{8,9},{9,8},{10,11... | collective-permute-start | bytes 1572872 | tf_op jit(solution)/shard_map/ppermute | solution.py:526
  60.7 8.0 %collective-permute-start.15 = (bf16[64,8,128]{2,1,0:T(8,128)(2,1)S(1)}, bf16[64,8,128]{2,1,0:T(8,128)(2,1)S(1)}, u32[]{:S(2)}, u32[]{:S(2)}) collective-permute-start(bf16[64,8,128]{2,1,0:T(8,128)(2,1)S(1)} %get-tuple-element.61.p0.sent.s0), channel_id=1, source_target_pairs={{0,31},{1,2},{2,1},{3,4},{4,3},{5,6},{6,5},{7,8},{8,7},{9,10},{10,... | collective-permute-start | bytes 393224 | tf_op jit(solution)/shard_map/ppermute | solution.py:522
  68.7 6.2 %collective-permute-start.16 = (bf16[64,8,128]{2,1,0:T(8,128)(2,1)S(1)}, bf16[64,8,128]{2,1,0:T(8,128)(2,1)S(1)}, u32[]{:S(2)}, u32[]{:S(2)}) collective-permute-start(bf16[64,8,128]{2,1,0:T(8,128)(2,1)S(1)} %collective-permute-done.15.p0), channel_id=1, source_target_pairs={{0,32},{32,64},{64,96},{96,0},{1,33},{33,65},{65,97},{97,1},{2,34}... | collective-permute-start | bytes 393224 | tf_op jit(solution)/shard_map/ppermute | solution.py:486
  69.5 7.5 %collective-permute-start.17 = (bf16[64,8,128]{2,1,0:T(8,128)(2,1)S(1)}, bf16[64,8,128]{2,1,0:T(8,128)(2,1)S(1)}, u32[]{:S(2)}, u32[]{:S(2)}) collective-permute-start(bf16[64,8,128]{2,1,0:T(8,128)(2,1)S(1)} %collective-permute-done.15.p0), channel_id=1, source_target_pairs={{0,64},{32,96},{64,0},{96,32},{1,65},{33,97},{65,1},{97,33},{2,66}... | collective-permute-start | bytes 393224 | tf_op jit(solution)/shard_map/ppermute | solution.py:486
  72.7 5.0 %collective-permute-start.18 = (bf16[64,8,128]{2,1,0:T(8,128)(2,1)S(1)}, bf16[64,8,128]{2,1,0:T(8,128)(2,1)S(1)}, u32[]{:S(2)}, u32[]{:S(2)}) collective-permute-start(bf16[64,8,128]{2,1,0:T(8,128)(2,1)S(1)} %collective-permute-done.15.p0), channel_id=1, source_target_pairs={{0,96},{32,0},{64,32},{96,64},{1,97},{33,1},{65,33},{97,65},{2,98}... | collective-permute-start | bytes 393224 | tf_op jit(solution)/shard_map/ppermute | solution.py:486
  80.1 12.0 %collective-permute-start.23 = (bf16[64,32,128]{2,1,0:T(8,128)(2,1)S(1)}, bf16[64,32,128]{2,1,0:T(8,128)(2,1)S(1)}, u32[]{:S(2)}, u32[]{:S(2)}) collective-permute-start(bf16[64,32,128]{2,1,0:T(8,128)(2,1)S(1)} %shard_map.65.own), channel_id=1, source_target_pairs={{0,31},{1,2},{2,1},{3,4},{4,3},{5,6},{6,5},{7,8},{8,7},{9,10},{10,... | collective-permute-start | bytes 1572872 | tf_op jit(solution)/shard_map/ppermute | solution.py:483
  83.1 9.0 %collective-permute-start.24 = (bf16[64,32,128]{2,1,0:T(8,128)(2,1)S(1)}, bf16[64,32,128]{2,1,0:T(8,128)(2,1)S(1)}, u32[]{:S(2)}, u32[]{:S(2)}) collective-permute-start(bf16[64,32,128]{2,1,0:T(8,128)(2,1)S(1)} %shard_map.65.own), channel_id=1, source_target_pairs={{0,1},{1,0},{2,3},{3,2},{4,5},{5,4},{6,7},{7,6},{8,9},{9,8},{10,11... | collective-permute-start | bytes 1572872 | tf_op jit(solution)/shard_map/ppermute | solution.py:483
  93.1 6.5 %collective-permute-start.25 = (bf16[512,128]{1,0:T(8,128)(2,1)S(1)}, bf16[512,128]{1,0:T(8,128)(2,1)S(1)}, u32[]{:S(2)}, u32[]{:S(2)}) collective-permute-start(bf16[512,128]{1,0:T(8,128)(2,1)S(1)} %get-tuple-element.65), channel_id=1, source_target_pairs={{0,32},{32,64},{64,96},{96,0},{1,33},{33,65},{65,97},{97,1},{2,34}... | collective-permute-start | bytes 393224 | tf_op jit(solution)/shard_map/ppermute | solution.py:505
  93.5 8.8 %collective-permute-start.26 = (bf16[512,128]{1,0:T(8,128)(2,1)S(1)}, bf16[512,128]{1,0:T(8,128)(2,1)S(1)}, u32[]{:S(2)}, u32[]{:S(2)}) collective-permute-start(bf16[512,128]{1,0:T(8,128)(2,1)S(1)} %get-tuple-element.66), channel_id=1, source_target_pairs={{0,64},{32,96},{64,0},{96,32},{1,65},{33,97},{65,1},{97,33},{2,66}... | collective-permute-start | bytes 393224 | tf_op jit(solution)/shard_map/ppermute | solution.py:505
  96.7 6.8 %collective-permute-start.27 = (bf16[512,128]{1,0:T(8,128)(2,1)S(1)}, bf16[512,128]{1,0:T(8,128)(2,1)S(1)}, u32[]{:S(2)}, u32[]{:S(2)}) collective-permute-start(bf16[512,128]{1,0:T(8,128)(2,1)S(1)} %get-tuple-element.67), channel_id=1, source_target_pairs={{0,96},{32,0},{64,32},{96,64},{1,97},{33,1},{65,33},{97,65},{2,98}... | collective-permute-start | bytes 393224 | tf_op jit(solution)/shard_map/ppermute | solution.py:505
  105.5 6.5 %collective-permute-start.28 = (f16[520,128]{1,0:T(8,128)(2,1)S(1)}, f16[520,128]{1,0:T(8,128)(2,1)S(1)}, u32[]{:S(2)}, u32[]{:S(2)}) collective-permute-start(f16[520,128]{1,0:T(8,128)(2,1)S(1)} %convert_element_type.17), channel_id=1, source_target_pairs={{0,32},{32,64},{64,96},{96,0},{1,33},{33,65},{65,97},{97,1},{2,34}... | collective-permute-start | bytes 399368 | tf_op jit(solution)/shard_map/ppermute | solution.py:486
  107.3 7.6 %collective-permute-start.29 = (f16[520,128]{1,0:T(8,128)(2,1)S(1)}, f16[520,128]{1,0:T(8,128)(2,1)S(1)}, u32[]{:S(2)}, u32[]{:S(2)}) collective-permute-start(f16[520,128]{1,0:T(8,128)(2,1)S(1)} %convert_element_type.17), channel_id=1, source_target_pairs={{0,64},{32,96},{64,0},{96,32},{1,65},{33,97},{65,1},{97,33},{2,66}... | collective-permute-start | bytes 399368 | tf_op jit(solution)/shard_map/ppermute | solution.py:486
  110.5 5.0 %collective-permute-start.30 = (f16[520,128]{1,0:T(8,128)(2,1)S(1)}, f16[520,128]{1,0:T(8,128)(2,1)S(1)}, u32[]{:S(2)}, u32[]{:S(2)}) collective-permute-start(f16[520,128]{1,0:T(8,128)(2,1)S(1)} %convert_element_type.17), channel_id=1, source_target_pairs={{0,96},{32,0},{64,32},{96,64},{1,97},{33,1},{65,33},{97,65},{2,98}... | collective-permute-start | bytes 399368 | tf_op jit(solution)/shard_map/ppermute | solution.py:486
  115.6 2.0 %collective-permute-start.31 = (f32[4,32,8,128]{3,2,1,0:T(8,128)S(1)}, f32[4,32,8,128]{3,2,1,0:T(8,128)S(1)}, u32[]{:S(2)}, u32[]{:S(2)}) collective-permute-start(f32[4,32,8,128]{3,2,1,0:T(8,128)S(1)} %shard_map.68), channel_id=1, source_target_pairs={{0,1},{1,0},{2,3},{3,2},{4,5},{5,4},{6,7},{7,6},{8,9},{9,8},{10,11... | collective-permute-start | bytes 1572872 | tf_op jit(solution)/shard_map/ppermute | solution.py:541
  (7 other events, 43.0 us)
where the time goes:
time: 120 us; the launch traced here: 119 us
  starting transfers between devices  53.6 us (45%)
  waiting for transfers between devices  46.1 us (38%)
  Pallas kernels  16.6 us (14%)
  local copies, waits for them, and re-layouts  2.14 us (2%)
    ppermute x12, starting transfers between devices, from_views(): lax.ppermute(x, 'view', steps(VIEWS, i))  18.3 us
    ppermute x12, waiting for transfers between devices, from_views(): lax.ppermute(x, 'view', steps(VIEWS, i))  17.3 us
    pallas_call x15, Pallas kernels, run(): pl.pallas_call(kernel, out_shape=shapes, in_specs=specs, out_specs=[pl.Bl...  16.6 us
    ppermute x6, waiting for transfers between devices, on_device(): lax.ppermute(parts[i], 'view', steps(VIEWS, i))  11.3 us
    ppermute x6, starting transfers between devices, on_device(): lax.ppermute(parts[i], 'view', steps(VIEWS, i))  9.2 us
    ppermute x4, waiting for transfers between devices, neighbours(): return (lax.ppermute(x, STRIPS, across), lax.ppermute(x, 'gz', swap))  8.99 us
    ppermute x4, starting transfers between devices, neighbours(): return (lax.ppermute(x, STRIPS, across), lax.ppermute(x, 'gz', swap))  7.47 us
    ppermute x1, starting transfers between devices, on_device(): lax.ppermute(vm, STRIPS, inward)  5.86 us
  transfers between devices with their start and end apart: 32, of which 21 were waited for; matrix products, arithmetic and copies ran while one was open for 0% of the time, Pallas kernels for 5%

commit v1 on v0

--- a/solution.py
+++ b/solution.py
@@ -286,7 +286,8 @@
     loop(FLAT // CHUNK, body)
 
 
-def back_y_kernel(far, own, near, yb, _, o0, o1, o2, o3, t):
+def back_y_kernel(far, own, near, yb, *refs):
+    o0, o1, o2, o3, t = refs[-5:]
     y_stage(strips_pair(far, own, near), yb[:, 0:SPAN], filtered_rows(t))
     v = lax.axis_index("view")
     for i, out in enumerate((o0, o1, o2, o3)):
@@ -445,8 +446,9 @@
     swap = steps(2, 1)
     e_far = [lax.ppermute(eo, STRIPS, outward), lax.ppermute(em, STRIPS, inward)]
     e_all = [eb, lax.ppermute(eb, "gz", swap)] + e_far
+    v_inside = lax.ppermute(views[0], "gz", swap)
     v_far = [lax.ppermute(vo, STRIPS, outward), lax.ppermute(vm, STRIPS, inward)]
-    v_all = [views[0], lax.ppermute(views[0], "gz", swap)] + v_far
+    v_all = [views[0], v_inside] + v_far
 
     yw, yf, yb, zf, x1f, x2f, yd, xd = call(
         own_mats_kernel,
@@ -487,6 +489,7 @@
 
     late, theirs, _ = lax.optimization_barrier((taps, theirs, ratio))
     theirs = lax.ppermute(theirs, "gz", swap)
+    every = from_views(late)
     zb, x1b, x2b = call(
         all_mats_kernel,
         [
@@ -495,12 +498,14 @@
             arr((VIEWS * WIDTH, WIDTH), BF16),
         ],
         smem=(4,),
-    )(*from_views(late), coverage)
+    )(*every, coverage)
 
     field = None
     for step in range(ITERS):
         far, near = neighbours(ratio)
-        parts = call(back_y_kernel, [arr(quart, BF16)] * VIEWS, [flat])(far, ratio, near, yb, zb)
+        parts = call(back_y_kernel, [arr(quart, BF16)] * VIEWS, [flat])(
+            far, ratio, near, yb, *(every[1:] if step == 0 else ())
+        )
         terms = [parts[0]] + [
             lax.ppermute(parts[i], "view", steps(VIEWS, i)) for i in range(1, VIEWS)
         ]

time: 120 us -> 119 us (level)
  waiting for transfers between devices: 46.1 us -> 44.2 us
    ppermute x6, waiting for transfers between devices: 11.3 us -> 9.6 us  [on_device(): lax.ppermute(parts[i], 'view', steps(VIEWS, i))]
where the time goes in v1:
time: 119 us; the launch traced here: 118 us
  starting transfers between devices  54.3 us (46%)
  waiting for transfers between devices  44.2 us (37%)
  Pallas kernels  16.6 us (14%)
  local copies, waits for them, and re-layouts  2.14 us (2%)
    ppermute x12, starting transfers between devices, from_views(): lax.ppermute(x, 'view', steps(VIEWS, i))  18.4 us
    ppermute x12, waiting for transfers between devices, from_views(): lax.ppermute(x, 'view', steps(VIEWS, i))  17.4 us
    pallas_call x15, Pallas kernels, run(): pl.pallas_call(kernel, out_shape=shapes, in_specs=specs, out_specs=[pl.Bl...  16.6 us
    ppermute x6, starting transfers between devices, on_device(): lax.ppermute(parts[i], 'view', steps(VIEWS, i))  9.62 us
    ppermute x6, waiting for transfers between devices, on_device(): lax.ppermute(parts[i], 'view', steps(VIEWS, i))  9.6 us
    ppermute x4, waiting for transfers between devices, neighbours(): return (lax.ppermute(x, STRIPS, across), lax.ppermute(x, 'gz', swap))  8.9 us
    ppermute x4, starting transfers between devices, neighbours(): return (lax.ppermute(x, STRIPS, across), lax.ppermute(x, 'gz', swap))  7.55 us
    ppermute x1, starting transfers between devices, on_device(): lax.ppermute(vm, STRIPS, inward)  5.86 us
  transfers between devices with their start and end apart: 32, of which 21 were waited for; matrix products, arithmetic and copies ran while one was open for 0% of the time, Pallas kernels for 5%

profile of v1, /device:TPU:0, one launch (start us, length us, event | category | flops | bytes accessed | tf_op | source)
XLA Modules:
  0.0 117.6 jit_solution(2199609950181814842)
XLA Ops:
  2.1 1.7 %collective-permute-start.4 = (bf16[32,32,128]{2,1,0:T(8,128)(2,1)S(1)}, bf16[32,32,128]{2,1,0:T(8,128)(2,1)S(1)}, u32[]{:S(2)}, u32[]{:S(2)}) collective-permute-start(bf16[32,32,128]{2,1,0:T(8,128)(2,1)S(1)} %get-tuple-element.42), channel_id=1, source_target_pairs={{0,2},{1,31},{2,4},{3,1},{4,6},{5,3},{6,8},{7,5},{8,10},{9,7},{10,... | collective-permute-start | bytes 786440 | tf_op jit(solution)/shard_map/ppermute | solution.py:447
  3.8 5.1 %collective-permute-start = (bf16[32,64,128]{2,1,0:T(8,128)(2,1)S(1)}, bf16[32,64,128]{2,1,0:T(8,128)(2,1)S(1)}, u32[]{:S(2)}, u32[]{:S(2)}) collective-permute-start(bf16[32,64,128]{2,1,0:T(8,128)(2,1)S(1)} %bitcast.6), channel_id=1, source_target_pairs={{0,1},{1,0},{2,3},{3,2},{4,5},{5,4},{6,7},{7,6},{8,9},{9,8},{10,11... | collective-permute-start | bytes 1572872 | tf_op jit(solution)/shard_map/ppermute | solution.py:449
  11.5 1.6 %collective-permute-done.4.far_a = bf16[32,32,128]{2,1,0:T(8,128)(2,1)S(1)} collective-permute-done((bf16[32,32,128]{2,1,0:T(8,128)(2,1)S(1)}, bf16[32,32,128]{2,1,0:T(8,128)(2,1)S(1)}, u32[]{:S(2)}, u32[]{:S(2)}) %collective-permute-start.4) | collective-permute-done | bytes 262176 | tf_op jit(solution)/shard_map/ppermute | solution.py:447
  13.1 5.9 %collective-permute-start.2 = (bf16[32,32,128]{2,1,0:T(8,128)(2,1)}, bf16[32,32,128]{2,1,0:T(8,128)(2,1)S(1)}, u32[]{:S(2)}, u32[]{:S(2)}) collective-permute-start(bf16[32,32,128]{2,1,0:T(8,128)(2,1)} %get-tuple-element.38), channel_id=1, source_target_pairs={{0,31},{1,2},{2,1},{3,4},{4,3},{5,6},{6,5},{7,8},{8,7},{9,10},{10,... | collective-permute-start | bytes 786440 | tf_op jit(solution)/shard_map/ppermute | solution.py:450
  20.5 2.3 %shard_map.58.pred = f32[2048,128]{1,0:T(8,128)S(1)} custom-call(bf16[32,64,128]{2,1,0:T(8,128)(2,1)S(1)} %get-tuple-element.41.slab, bf16[32,64,128]{2,1,0:T(8,128)(2,1)S(1)} %collective-permute-done.3.other, bf16[32,32,128]{2,1,0:T(8,128)(2,1)S(1)} %collective-permute-done.4.far_a, bf16[32,32,128]{2,1,0:T(8,128)(2,1)S(1)} %collective-permute-done.5.far_b, ...), custom_call_target="tpu_custom_call" | custom-call | flops 100000000 | bytes 4194304 | tf_op jit(solution)/shard_map/pallas_call | solution.py:46
  25.2 4.4 %collective-permute-start.6 = (bf16[64,32,128]{2,1,0:T(8,128)(2,1)S(1)}, bf16[64,32,128]{2,1,0:T(8,128)(2,1)S(1)}, u32[]{:S(2)}, u32[]{:S(2)}) collective-permute-start(bf16[64,32,128]{2,1,0:T(8,128)(2,1)S(1)} %get-tuple-element.48.own), channel_id=1, source_target_pairs={{0,31},{1,2},{2,1},{3,4},{4,3},{5,6},{6,5},{7,8},{8,7},{9,10},{10,... | collective-permute-start | bytes 1572872 | tf_op jit(solution)/shard_map/ppermute | solution.py:485
  29.7 2.8 %collective-permute-start.10 = (f32[8,128]{1,0:T(8,128)S(1)}, f32[8,128]{1,0:T(8,128)S(1)}, u32[]{:S(2)}, u32[]{:S(2)}) collective-permute-start(f32[8,128]{1,0:T(8,128)S(1)} %select_maximum_fusion.taps.t0), channel_id=1, source_target_pairs={{0,96},{32,0},{64,32},{96,64},{1,97},{33,1},{65,33},{97,65},{2,98}... | collective-permute-start | bytes 12296 | tf_op jit(solution)/shard_map/ppermute | solution.py:488
  32.4 2.3 %collective-permute-start.9 = (f32[8,128]{1,0:T(8,128)S(1)}, f32[8,128]{1,0:T(8,128)S(1)}, u32[]{:S(2)}, u32[]{:S(2)}) collective-permute-start(f32[8,128]{1,0:T(8,128)S(1)} %select_maximum_fusion.taps.t0), channel_id=1, source_target_pairs={{0,64},{32,96},{64,0},{96,32},{1,65},{33,97},{65,1},{97,33},{2,66}... | collective-permute-start | bytes 12296 | tf_op jit(solution)/shard_map/ppermute | solution.py:488
  34.7 2.5 %collective-permute-done.8.refs_0_.t1 = f32[8,128]{1,0:T(8,128)S(1)} collective-permute-done((f32[8,128]{1,0:T(8,128)S(1)}, f32[8,128]{1,0:T(8,128)S(1)}, u32[]{:S(2)}, u32[]{:S(2)}) %collective-permute-start.8) | collective-permute-done | bytes 4128 | tf_op jit(solution)/shard_map/ppermute | solution.py:488
  39.8 3.5 %collective-permute-start.12 = (bf16[512,128]{1,0:T(8,128)(2,1)S(1)}, bf16[512,128]{1,0:T(8,128)(2,1)S(1)}, u32[]{:S(2)}, u32[]{:S(2)}) collective-permute-start(bf16[512,128]{1,0:T(8,128)(2,1)S(1)} %get-tuple-element.54), channel_id=1, source_target_pairs={{0,64},{32,96},{64,0},{96,32},{1,65},{33,97},{65,1},{97,33},{2,66}... | collective-permute-start | bytes 393224 | tf_op jit(solution)/shard_map/ppermute | solution.py:510
  45.7 2.9 %collective-permute-done.12.t2 = bf16[512,128]{1,0:T(8,128)(2,1)S(1)} collective-permute-done((bf16[512,128]{1,0:T(8,128)(2,1)S(1)}, bf16[512,128]{1,0:T(8,128)(2,1)S(1)}, u32[]{:S(2)}, u32[]{:S(2)}) %collective-permute-start.12) | collective-permute-done | bytes 131104 | tf_op jit(solution)/shard_map/ppermute | solution.py:510
  48.6 1.8 %shard_map.62 = (f32[512,128]{1,0:T(8,128)S(1)}, bf16[64,8,128]{2,1,0:T(8,128)(2,1)S(1)}) custom-call(bf16[512,128]{1,0:T(8,128)(2,1)S(1)} %get-tuple-element.52.t0, bf16[512,128]{1,0:T(8,128)(2,1)S(1)} %collective-permute-done.11.t1, bf16[512,128]{1,0:T(8,128)(2,1)S(1)} %collective-permute-done.12.t2, bf16[512,128]{1,0:T(8,128)(2,1)S(1)} %collective-permute-done.13.t3, ...), custom_call_target="tpu_custom_call" | custom-call | flops 100000000 | bytes 4194304 | tf_op jit(solution)/shard_map/pallas_call | solution.py:46
  51.2 2.8 %collective-permute-start.20 = (bf16[64,8,128]{2,1,0:T(8,128)(2,1)S(1)}, bf16[64,8,128]{2,1,0:T(8,128)(2,1)S(1)}, u32[]{:S(2)}, u32[]{:S(2)}) collective-permute-start(bf16[64,8,128]{2,1,0:T(8,128)(2,1)S(1)} %get-tuple-element.61.p0.sent.s0), channel_id=1, source_target_pairs={{0,64},{32,96},{64,0},{96,32},{1,65},{33,97},{65,1},{97,33},{2,66}... | collective-permute-start | bytes 393224 | tf_op jit(solution)/shard_map/ppermute | solution.py:488
  54.5 2.9 %collective-permute-done.19.p1.s1 = bf16[64,8,128]{2,1,0:T(8,128)(2,1)S(1)} collective-permute-done((bf16[64,8,128]{2,1,0:T(8,128)(2,1)S(1)}, bf16[64,8,128]{2,1,0:T(8,128)(2,1)S(1)}, u32[]{:S(2)}, u32[]{:S(2)}) %collective-permute-start.19) | collective-permute-done | bytes 131104 | tf_op jit(solution)/shard_map/ppermute | solution.py:488
  59.5 4.2 %collective-permute-start.15 = (bf16[64,8,128]{2,1,0:T(8,128)(2,1)S(1)}, bf16[64,8,128]{2,1,0:T(8,128)(2,1)S(1)}, u32[]{:S(2)}, u32[]{:S(2)}) collective-permute-start(bf16[64,8,128]{2,1,0:T(8,128)(2,1)S(1)} %get-tuple-element.61.p0.sent.s0), channel_id=1, source_target_pairs={{0,31},{1,2},{2,1},{3,4},{4,3},{5,6},{6,5},{7,8},{8,7},{9,10},{10,... | collective-permute-start | bytes 393224 | tf_op jit(solution)/shard_map/ppermute | solution.py:527
  63.8 3.7 %collective-permute-done.15.p0 = bf16[64,8,128]{2,1,0:T(8,128)(2,1)S(1)} collective-permute-done((bf16[64,8,128]{2,1,0:T(8,128)(2,1)S(1)}, bf16[64,8,128]{2,1,0:T(8,128)(2,1)S(1)}, u32[]{:S(2)}, u32[]{:S(2)}) %collective-permute-start.15) | collective-permute-done | bytes 131104 | tf_op jit(solution)/shard_map/ppermute | solution.py:527
  68.2 3.4 %collective-permute-start.17 = (bf16[64,8,128]{2,1,0:T(8,128)(2,1)S(1)}, bf16[64,8,128]{2,1,0:T(8,128)(2,1)S(1)}, u32[]{:S(2)}, u32[]{:S(2)}) collective-permute-start(bf16[64,8,128]{2,1,0:T(8,128)(2,1)S(1)} %collective-permute-done.15.p0), channel_id=1, source_target_pairs={{0,64},{32,96},{64,0},{96,32},{1,65},{33,97},{65,1},{97,33},{2,66}... | collective-permute-start | bytes 393224 | tf_op jit(solution)/shard_map/ppermute | solution.py:488
  71.6 2.0 %collective-permute-done.16.p1 = bf16[64,8,128]{2,1,0:T(8,128)(2,1)S(1)} collective-permute-done((bf16[64,8,128]{2,1,0:T(8,128)(2,1)S(1)}, bf16[64,8,128]{2,1,0:T(8,128)(2,1)S(1)}, u32[]{:S(2)}, u32[]{:S(2)}) %collective-permute-start.16) | collective-permute-done | bytes 131104 | tf_op jit(solution)/shard_map/ppermute | solution.py:488
  73.7 2.3 %collective-permute-done.17.p2 = bf16[64,8,128]{2,1,0:T(8,128)(2,1)S(1)} collective-permute-done((bf16[64,8,128]{2,1,0:T(8,128)(2,1)S(1)}, bf16[64,8,128]{2,1,0:T(8,128)(2,1)S(1)}, u32[]{:S(2)}, u32[]{:S(2)}) %collective-permute-start.17) | collective-permute-done | bytes 131104 | tf_op jit(solution)/shard_map/ppermute | solution.py:488
  76.8 2.2 %shard_map.65.own = bf16[64,32,128]{2,1,0:T(8,128)(2,1)S(1)} custom-call(bf16[64,32,128]{2,1,0:T(8,128)(2,1)S(1)} %shard_map.63.far, bf16[64,32,128]{2,1,0:T(8,128)(2,1)S(1)} %shard_map.64.own, bf16[64,32,128]{2,1,0:T(8,128)(2,1)S(1)} %collective-permute-done.22.near, bf16[64,128]{1,0:T(8,128)(2,1)S(1)} %get-tuple-element.62.yf, ...), custom_call_target="tpu_custom_call" | custom-call | flops 100000000 | bytes 4194304 | tf_op jit(solution)/shard_map/pallas_call | solution.py:46
  79.0 3.1 %collective-permute-start.23 = (bf16[64,32,128]{2,1,0:T(8,128)(2,1)S(1)}, bf16[64,32,128]{2,1,0:T(8,128)(2,1)S(1)}, u32[]{:S(2)}, u32[]{:S(2)}) collective-permute-start(bf16[64,32,128]{2,1,0:T(8,128)(2,1)S(1)} %shard_map.65.own), channel_id=1, source_target_pairs={{0,31},{1,2},{2,1},{3,4},{4,3},{5,6},{6,5},{7,8},{8,7},{9,10},{10,... | collective-permute-start | bytes 1572872 | tf_op jit(solution)/shard_map/ppermute | solution.py:485
  82.1 8.9 %collective-permute-done.23.far = bf16[64,32,128]{2,1,0:T(8,128)(2,1)S(1)} collective-permute-done((bf16[64,32,128]{2,1,0:T(8,128)(2,1)S(1)}, bf16[64,32,128]{2,1,0:T(8,128)(2,1)S(1)}, u32[]{:S(2)}, u32[]{:S(2)}) %collective-permute-start.23) | collective-permute-done | bytes 524320 | tf_op jit(solution)/shard_map/ppermute | solution.py:485
  92.2 3.4 %collective-permute-start.26 = (bf16[512,128]{1,0:T(8,128)(2,1)S(1)}, bf16[512,128]{1,0:T(8,128)(2,1)S(1)}, u32[]{:S(2)}, u32[]{:S(2)}) collective-permute-start(bf16[512,128]{1,0:T(8,128)(2,1)S(1)} %get-tuple-element.66), channel_id=1, source_target_pairs={{0,64},{32,96},{64,0},{96,32},{1,65},{33,97},{65,1},{97,33},{2,66}... | collective-permute-start | bytes 393224 | tf_op jit(solution)/shard_map/ppermute | solution.py:510
  96.2 2.2 %collective-permute-done.25.t1 = bf16[512,128]{1,0:T(8,128)(2,1)S(1)} collective-permute-done((bf16[512,128]{1,0:T(8,128)(2,1)S(1)}, bf16[512,128]{1,0:T(8,128)(2,1)S(1)}, u32[]{:S(2)}, u32[]{:S(2)}) %collective-permute-start.25) | collective-permute-done | bytes 131104 | tf_op jit(solution)/shard_map/ppermute | solution.py:510
  98.4 2.4 %collective-permute-done.26.t2 = bf16[512,128]{1,0:T(8,128)(2,1)S(1)} collective-permute-done((bf16[512,128]{1,0:T(8,128)(2,1)S(1)}, bf16[512,128]{1,0:T(8,128)(2,1)S(1)}, u32[]{:S(2)}, u32[]{:S(2)}) %collective-permute-start.26) | collective-permute-done | bytes 131104 | tf_op jit(solution)/shard_map/ppermute | solution.py:510
  100.9 1.5 %collective-permute-done.27.t3 = bf16[512,128]{1,0:T(8,128)(2,1)S(1)} collective-permute-done((bf16[512,128]{1,0:T(8,128)(2,1)S(1)}, bf16[512,128]{1,0:T(8,128)(2,1)S(1)}, u32[]{:S(2)}, u32[]{:S(2)}) %collective-permute-start.27) | collective-permute-done | bytes 131104 | tf_op jit(solution)/shard_map/ppermute | solution.py:510
  102.4 1.9 %shard_map.67 = f32[520,128]{1,0:T(8,128)S(1)} custom-call(bf16[512,128]{1,0:T(8,128)(2,1)S(1)} %get-tuple-element.64.t0, bf16[512,128]{1,0:T(8,128)(2,1)S(1)} %collective-permute-done.25.t1, bf16[512,128]{1,0:T(8,128)(2,1)S(1)} %collective-permute-done.26.t2, bf16[512,128]{1,0:T(8,128)(2,1)S(1)} %collective-permute-done.27.t3, ...), custom_call_target="tpu_custom_call" | custom-call | flops 100000000 | bytes 4194304 | tf_op jit(solution)/shard_map/pallas_call | solution.py:46
  104.3 1.9 %collective-permute-start.28 = (f16[520,128]{1,0:T(8,128)(2,1)S(1)}, f16[520,128]{1,0:T(8,128)(2,1)S(1)}, u32[]{:S(2)}, u32[]{:S(2)}) collective-permute-start(f16[520,128]{1,0:T(8,128)(2,1)S(1)} %convert_element_type.17), channel_id=1, source_target_pairs={{0,32},{32,64},{64,96},{96,0},{1,33},{33,65},{65,97},{97,1},{2,34}... | collective-permute-start | bytes 399368 | tf_op jit(solution)/shard_map/ppermute | solution.py:488
  106.2 3.2 %collective-permute-start.29 = (f16[520,128]{1,0:T(8,128)(2,1)S(1)}, f16[520,128]{1,0:T(8,128)(2,1)S(1)}, u32[]{:S(2)}, u32[]{:S(2)}) collective-permute-start(f16[520,128]{1,0:T(8,128)(2,1)S(1)} %convert_element_type.17), channel_id=1, source_target_pairs={{0,64},{32,96},{64,0},{96,32},{1,65},{33,97},{65,1},{97,33},{2,66}... | collective-permute-start | bytes 399368 | tf_op jit(solution)/shard_map/ppermute | solution.py:488
  109.4 1.5 %collective-permute-done.28 = f16[520,128]{1,0:T(8,128)(2,1)S(1)} collective-permute-done((f16[520,128]{1,0:T(8,128)(2,1)S(1)}, f16[520,128]{1,0:T(8,128)(2,1)S(1)}, u32[]{:S(2)}, u32[]{:S(2)}) %collective-permute-start.28) | collective-permute-done | bytes 133152 | tf_op jit(solution)/shard_map/ppermute | solution.py:488
  110.9 2.9 %collective-permute-done.29 = f16[520,128]{1,0:T(8,128)(2,1)S(1)} collective-permute-done((f16[520,128]{1,0:T(8,128)(2,1)S(1)}, f16[520,128]{1,0:T(8,128)(2,1)S(1)}, u32[]{:S(2)}, u32[]{:S(2)}) %collective-permute-start.29) | collective-permute-done | bytes 133152 | tf_op jit(solution)/shard_map/ppermute | solution.py:488
  114.6 1.9 %collective-permute-done.31.got = f32[4,32,8,128]{3,2,1,0:T(8,128)S(1)} collective-permute-done((f32[4,32,8,128]{3,2,1,0:T(8,128)S(1)}, f32[4,32,8,128]{3,2,1,0:T(8,128)S(1)}, u32[]{:S(2)}, u32[]{:S(2)}) %collective-permute-start.31) | collective-permute-done | bytes 524320 | tf_op jit(solution)/shard_map/ppermute | solution.py:546
  (70 shorter events, 22.3 us)
Async XLA Ops:
  2.1 18.4 %collective-permute-start.3 = (bf16[32,64,128]{2,1,0:T(8,128)(2,1)S(1)}, bf16[32,64,128]{2,1,0:T(8,128)(2,1)S(1)}, u32[]{:S(2)}, u32[]{:S(2)}) collective-permute-start(bf16[32,64,128]{2,1,0:T(8,128)(2,1)S(1)} %get-tuple-element.41.slab), channel_id=1, source_target_pairs={{0,1},{1,0},{2,3},{3,2},{4,5},{5,4},{6,7},{7,6},{8,9},{9,8},{10,11... | collective-permute-start | bytes 1572872 | tf_op jit(solution)/shard_map/ppermute | solution.py:448
  2.1 10.9 %collective-permute-start.4 = (bf16[32,32,128]{2,1,0:T(8,128)(2,1)S(1)}, bf16[32,32,128]{2,1,0:T(8,128)(2,1)S(1)}, u32[]{:S(2)}, u32[]{:S(2)}) collective-permute-start(bf16[32,32,128]{2,1,0:T(8,128)(2,1)S(1)} %get-tuple-element.42), channel_id=1, source_target_pairs={{0,2},{1,31},{2,4},{3,1},{4,6},{5,3},{6,8},{7,5},{8,10},{9,7},{10,... | collective-permute-start | bytes 786440 | tf_op jit(solution)/shard_map/ppermute | solution.py:447
  3.8 20.1 %collective-permute-start = (bf16[32,64,128]{2,1,0:T(8,128)(2,1)S(1)}, bf16[32,64,128]{2,1,0:T(8,128)(2,1)S(1)}, u32[]{:S(2)}, u32[]{:S(2)}) collective-permute-start(bf16[32,64,128]{2,1,0:T(8,128)(2,1)S(1)} %bitcast.6), channel_id=1, source_target_pairs={{0,1},{1,0},{2,3},{3,2},{4,5},{5,4},{6,7},{7,6},{8,9},{9,8},{10,11... | collective-permute-start | bytes 1572872 | tf_op jit(solution)/shard_map/ppermute | solution.py:449
  9.0 11.5 %collective-permute-start.5 = (bf16[32,32,128]{2,1,0:T(8,128)(2,1)}, bf16[32,32,128]{2,1,0:T(8,128)(2,1)S(1)}, u32[]{:S(2)}, u32[]{:S(2)}) collective-permute-start(bf16[32,32,128]{2,1,0:T(8,128)(2,1)} %get-tuple-element.43), channel_id=1, source_target_pairs={{0,31},{1,2},{2,1},{3,4},{4,3},{5,6},{6,5},{7,8},{8,7},{9,10},{10,... | collective-permute-start | bytes 786440 | tf_op jit(solution)/shard_map/ppermute | solution.py:447
  10.2 12.6 %collective-permute-start.1 = (bf16[32,32,128]{2,1,0:T(8,128)(2,1)}, bf16[32,32,128]{2,1,0:T(8,128)(2,1)S(1)}, u32[]{:S(2)}, u32[]{:S(2)}) collective-permute-start(bf16[32,32,128]{2,1,0:T(8,128)(2,1)} %get-tuple-element.37), channel_id=1, source_target_pairs={{0,2},{1,31},{2,4},{3,1},{4,6},{5,3},{6,8},{7,5},{8,10},{9,7},{10,... | collective-permute-start | bytes 786440 | tf_op jit(solution)/shard_map/ppermute | solution.py:450
  13.1 10.8 %collective-permute-start.2 = (bf16[32,32,128]{2,1,0:T(8,128)(2,1)}, bf16[32,32,128]{2,1,0:T(8,128)(2,1)S(1)}, u32[]{:S(2)}, u32[]{:S(2)}) collective-permute-start(bf16[32,32,128]{2,1,0:T(8,128)(2,1)} %get-tuple-element.38), channel_id=1, source_target_pairs={{0,31},{1,2},{2,1},{3,4},{4,3},{5,6},{6,5},{7,8},{8,7},{9,10},{10,... | collective-permute-start | bytes 786440 | tf_op jit(solution)/shard_map/ppermute | solution.py:450
  25.2 12.3 %collective-permute-start.6 = (bf16[64,32,128]{2,1,0:T(8,128)(2,1)S(1)}, bf16[64,32,128]{2,1,0:T(8,128)(2,1)S(1)}, u32[]{:S(2)}, u32[]{:S(2)}) collective-permute-start(bf16[64,32,128]{2,1,0:T(8,128)(2,1)S(1)} %get-tuple-element.48.own), channel_id=1, source_target_pairs={{0,31},{1,2},{2,1},{3,4},{4,3},{5,6},{6,5},{7,8},{8,7},{9,10},{10,... | collective-permute-start | bytes 1572872 | tf_op jit(solution)/shard_map/ppermute | solution.py:485
  29.7 7.9 %collective-permute-start.7 = (bf16[64,32,128]{2,1,0:T(8,128)(2,1)S(1)}, bf16[64,32,128]{2,1,0:T(8,128)(2,1)S(1)}, u32[]{:S(2)}, u32[]{:S(2)}) collective-permute-start(bf16[64,32,128]{2,1,0:T(8,128)(2,1)S(1)} %get-tuple-element.48.own), channel_id=1, source_target_pairs={{0,1},{1,0},{2,3},{3,2},{4,5},{5,4},{6,7},{7,6},{8,9},{9,8},{10,11... | collective-permute-start | bytes 1572872 | tf_op jit(solution)/shard_map/ppermute | solution.py:485
  29.7 5.0 %collective-permute-start.10 = (f32[8,128]{1,0:T(8,128)S(1)}, f32[8,128]{1,0:T(8,128)S(1)}, u32[]{:S(2)}, u32[]{:S(2)}) collective-permute-start(f32[8,128]{1,0:T(8,128)S(1)} %select_maximum_fusion.taps.t0), channel_id=1, source_target_pairs={{0,96},{32,0},{64,32},{96,64},{1,97},{33,1},{65,33},{97,65},{2,98}... | collective-permute-start | bytes 12296 | tf_op jit(solution)/shard_map/ppermute | solution.py:488
  32.4 4.8 %collective-permute-start.8 = (f32[8,128]{1,0:T(8,128)S(1)}, f32[8,128]{1,0:T(8,128)S(1)}, u32[]{:S(2)}, u32[]{:S(2)}) collective-permute-start(f32[8,128]{1,0:T(8,128)S(1)} %select_maximum_fusion.taps.t0), channel_id=1, source_target_pairs={{0,32},{32,64},{64,96},{96,0},{1,33},{33,65},{65,97},{97,1},{2,34}... | collective-permute-start | bytes 12296 | tf_op jit(solution)/shard_map/ppermute | solution.py:488
  32.4 5.1 %collective-permute-start.9 = (f32[8,128]{1,0:T(8,128)S(1)}, f32[8,128]{1,0:T(8,128)S(1)}, u32[]{:S(2)}, u32[]{:S(2)}) collective-permute-start(f32[8,128]{1,0:T(8,128)S(1)} %select_maximum_fusion.taps.t0), channel_id=1, source_target_pairs={{0,64},{32,96},{64,0},{96,32},{1,65},{33,97},{65,1},{97,33},{2,66}... | collective-permute-start | bytes 12296 | tf_op jit(solution)/shard_map/ppermute | solution.py:488
  34.7 10.4 %collective-permute-start.14 = (f32[32,8,128]{2,1,0:T(8,128)S(1)}, f32[32,8,128]{2,1,0:T(8,128)S(1)}, u32[]{:S(2)}, u32[]{:S(2)}) collective-permute-start(f32[32,8,128]{2,1,0:T(8,128)S(1)} %copy-done.4), channel_id=1, source_target_pairs={{0,1},{1,0},{2,3},{3,2},{4,5},{5,4},{6,7},{7,6},{8,9},{9,8},{10,11... | collective-permute-start | bytes 393224 | tf_op jit(solution)/shard_map/ppermute | solution.py:491
  38.6 7.1 %collective-permute-start.11 = (bf16[512,128]{1,0:T(8,128)(2,1)S(1)}, bf16[512,128]{1,0:T(8,128)(2,1)S(1)}, u32[]{:S(2)}, u32[]{:S(2)}) collective-permute-start(bf16[512,128]{1,0:T(8,128)(2,1)S(1)} %get-tuple-element.53), channel_id=1, source_target_pairs={{0,32},{32,64},{64,96},{96,0},{1,33},{33,65},{65,97},{97,1},{2,34}... | collective-permute-start | bytes 393224 | tf_op jit(solution)/shard_map/ppermute | solution.py:510
  39.8 8.8 %collective-permute-start.12 = (bf16[512,128]{1,0:T(8,128)(2,1)S(1)}, bf16[512,128]{1,0:T(8,128)(2,1)S(1)}, u32[]{:S(2)}, u32[]{:S(2)}) collective-permute-start(bf16[512,128]{1,0:T(8,128)(2,1)S(1)} %get-tuple-element.54), channel_id=1, source_target_pairs={{0,64},{32,96},{64,0},{96,32},{1,65},{33,97},{65,1},{97,33},{2,66}... | collective-permute-start | bytes 393224 | tf_op jit(solution)/shard_map/ppermute | solution.py:510
  43.3 5.3 %collective-permute-start.13 = (bf16[512,128]{1,0:T(8,128)(2,1)S(1)}, bf16[512,128]{1,0:T(8,128)(2,1)S(1)}, u32[]{:S(2)}, u32[]{:S(2)}) collective-permute-start(bf16[512,128]{1,0:T(8,128)(2,1)S(1)} %get-tuple-element.55), channel_id=1, source_target_pairs={{0,96},{32,0},{64,32},{96,64},{1,97},{33,1},{65,33},{97,65},{2,98}... | collective-permute-start | bytes 393224 | tf_op jit(solution)/shard_map/ppermute | solution.py:510
  50.4 7.0 %collective-permute-start.19 = (bf16[64,8,128]{2,1,0:T(8,128)(2,1)S(1)}, bf16[64,8,128]{2,1,0:T(8,128)(2,1)S(1)}, u32[]{:S(2)}, u32[]{:S(2)}) collective-permute-start(bf16[64,8,128]{2,1,0:T(8,128)(2,1)S(1)} %get-tuple-element.61.p0.sent.s0), channel_id=1, source_target_pairs={{0,32},{32,64},{64,96},{96,0},{1,33},{33,65},{65,97},{97,1},{2,34}... | collective-permute-start | bytes 393224 | tf_op jit(solution)/shard_map/ppermute | solution.py:488
  51.2 7.6 %collective-permute-start.20 = (bf16[64,8,128]{2,1,0:T(8,128)(2,1)S(1)}, bf16[64,8,128]{2,1,0:T(8,128)(2,1)S(1)}, u32[]{:S(2)}, u32[]{:S(2)}) collective-permute-start(bf16[64,8,128]{2,1,0:T(8,128)(2,1)S(1)} %get-tuple-element.61.p0.sent.s0), channel_id=1, source_target_pairs={{0,64},{32,96},{64,0},{96,32},{1,65},{33,97},{65,1},{97,33},{2,66}... | collective-permute-start | bytes 393224 | tf_op jit(solution)/shard_map/ppermute | solution.py:488
  54.0 5.1 %collective-permute-start.21 = (bf16[64,8,128]{2,1,0:T(8,128)(2,1)S(1)}, bf16[64,8,128]{2,1,0:T(8,128)(2,1)S(1)}, u32[]{:S(2)}, u32[]{:S(2)}) collective-permute-start(bf16[64,8,128]{2,1,0:T(8,128)(2,1)S(1)} %get-tuple-element.61.p0.sent.s0), channel_id=1, source_target_pairs={{0,96},{32,0},{64,32},{96,64},{1,97},{33,1},{65,33},{97,65},{2,98}... | collective-permute-start | bytes 393224 | tf_op jit(solution)/shard_map/ppermute | solution.py:488
  59.4 17.4 %collective-permute-start.22 = (bf16[64,32,128]{2,1,0:T(8,128)(2,1)S(1)}, bf16[64,32,128]{2,1,0:T(8,128)(2,1)S(1)}, u32[]{:S(2)}, u32[]{:S(2)}) collective-permute-start(bf16[64,32,128]{2,1,0:T(8,128)(2,1)S(1)} %shard_map.64.own), channel_id=1, source_target_pairs={{0,1},{1,0},{2,3},{3,2},{4,5},{5,4},{6,7},{7,6},{8,9},{9,8},{10,11... | collective-permute-start | bytes 1572872 | tf_op jit(solution)/shard_map/ppermute | solution.py:531
  59.5 8.0 %collective-permute-start.15 = (bf16[64,8,128]{2,1,0:T(8,128)(2,1)S(1)}, bf16[64,8,128]{2,1,0:T(8,128)(2,1)S(1)}, u32[]{:S(2)}, u32[]{:S(2)}) collective-permute-start(bf16[64,8,128]{2,1,0:T(8,128)(2,1)S(1)} %get-tuple-element.61.p0.sent.s0), channel_id=1, source_target_pairs={{0,31},{1,2},{2,1},{3,4},{4,3},{5,6},{6,5},{7,8},{8,7},{9,10},{10,... | collective-permute-start | bytes 393224 | tf_op jit(solution)/shard_map/ppermute | solution.py:527
  67.5 6.2 %collective-permute-start.16 = (bf16[64,8,128]{2,1,0:T(8,128)(2,1)S(1)}, bf16[64,8,128]{2,1,0:T(8,128)(2,1)S(1)}, u32[]{:S(2)}, u32[]{:S(2)}) collective-permute-start(bf16[64,8,128]{2,1,0:T(8,128)(2,1)S(1)} %collective-permute-done.15.p0), channel_id=1, source_target_pairs={{0,32},{32,64},{64,96},{96,0},{1,33},{33,65},{65,97},{97,1},{2,34}... | collective-permute-start | bytes 393224 | tf_op jit(solution)/shard_map/ppermute | solution.py:488
  68.2 7.7 %collective-permute-start.17 = (bf16[64,8,128]{2,1,0:T(8,128)(2,1)S(1)}, bf16[64,8,128]{2,1,0:T(8,128)(2,1)S(1)}, u32[]{:S(2)}, u32[]{:S(2)}) collective-permute-start(bf16[64,8,128]{2,1,0:T(8,128)(2,1)S(1)} %collective-permute-done.15.p0), channel_id=1, source_target_pairs={{0,64},{32,96},{64,0},{96,32},{1,65},{33,97},{65,1},{97,33},{2,66}... | collective-permute-start | bytes 393224 | tf_op jit(solution)/shard_map/ppermute | solution.py:488
  71.6 5.0 %collective-permute-start.18 = (bf16[64,8,128]{2,1,0:T(8,128)(2,1)S(1)}, bf16[64,8,128]{2,1,0:T(8,128)(2,1)S(1)}, u32[]{:S(2)}, u32[]{:S(2)}) collective-permute-start(bf16[64,8,128]{2,1,0:T(8,128)(2,1)S(1)} %collective-permute-done.15.p0), channel_id=1, source_target_pairs={{0,96},{32,0},{64,32},{96,64},{1,97},{33,1},{65,33},{97,65},{2,98}... | collective-permute-start | bytes 393224 | tf_op jit(solution)/shard_map/ppermute | solution.py:488
  79.0 12.0 %collective-permute-start.23 = (bf16[64,32,128]{2,1,0:T(8,128)(2,1)S(1)}, bf16[64,32,128]{2,1,0:T(8,128)(2,1)S(1)}, u32[]{:S(2)}, u32[]{:S(2)}) collective-permute-start(bf16[64,32,128]{2,1,0:T(8,128)(2,1)S(1)} %shard_map.65.own), channel_id=1, source_target_pairs={{0,31},{1,2},{2,1},{3,4},{4,3},{5,6},{6,5},{7,8},{8,7},{9,10},{10,... | collective-permute-start | bytes 1572872 | tf_op jit(solution)/shard_map/ppermute | solution.py:485
  82.1 8.9 %collective-permute-start.24 = (bf16[64,32,128]{2,1,0:T(8,128)(2,1)S(1)}, bf16[64,32,128]{2,1,0:T(8,128)(2,1)S(1)}, u32[]{:S(2)}, u32[]{:S(2)}) collective-permute-start(bf16[64,32,128]{2,1,0:T(8,128)(2,1)S(1)} %shard_map.65.own), channel_id=1, source_target_pairs={{0,1},{1,0},{2,3},{3,2},{4,5},{5,4},{6,7},{7,6},{8,9},{9,8},{10,11... | collective-permute-start | bytes 1572872 | tf_op jit(solution)/shard_map/ppermute | solution.py:485
  92.0 6.4 %collective-permute-start.25 = (bf16[512,128]{1,0:T(8,128)(2,1)S(1)}, bf16[512,128]{1,0:T(8,128)(2,1)S(1)}, u32[]{:S(2)}, u32[]{:S(2)}) collective-permute-start(bf16[512,128]{1,0:T(8,128)(2,1)S(1)} %get-tuple-element.65), channel_id=1, source_target_pairs={{0,32},{32,64},{64,96},{96,0},{1,33},{33,65},{65,97},{97,1},{2,34}... | collective-permute-start | bytes 393224 | tf_op jit(solution)/shard_map/ppermute | solution.py:510
  92.2 8.7 %collective-permute-start.26 = (bf16[512,128]{1,0:T(8,128)(2,1)S(1)}, bf16[512,128]{1,0:T(8,128)(2,1)S(1)}, u32[]{:S(2)}, u32[]{:S(2)}) collective-permute-start(bf16[512,128]{1,0:T(8,128)(2,1)S(1)} %get-tuple-element.66), channel_id=1, source_target_pairs={{0,64},{32,96},{64,0},{96,32},{1,65},{33,97},{65,1},{97,33},{2,66}... | collective-permute-start | bytes 393224 | tf_op jit(solution)/shard_map/ppermute | solution.py:510
  95.5 6.8 %collective-permute-start.27 = (bf16[512,128]{1,0:T(8,128)(2,1)S(1)}, bf16[512,128]{1,0:T(8,128)(2,1)S(1)}, u32[]{:S(2)}, u32[]{:S(2)}) collective-permute-start(bf16[512,128]{1,0:T(8,128)(2,1)S(1)} %get-tuple-element.67), channel_id=1, source_target_pairs={{0,96},{32,0},{64,32},{96,64},{1,97},{33,1},{65,33},{97,65},{2,98}... | collective-permute-start | bytes 393224 | tf_op jit(solution)/shard_map/ppermute | solution.py:510
  104.3 6.6 %collective-permute-start.28 = (f16[520,128]{1,0:T(8,128)(2,1)S(1)}, f16[520,128]{1,0:T(8,128)(2,1)S(1)}, u32[]{:S(2)}, u32[]{:S(2)}) collective-permute-start(f16[520,128]{1,0:T(8,128)(2,1)S(1)} %convert_element_type.17), channel_id=1, source_target_pairs={{0,32},{32,64},{64,96},{96,0},{1,33},{33,65},{65,97},{97,1},{2,34}... | collective-permute-start | bytes 399368 | tf_op jit(solution)/shard_map/ppermute | solution.py:488
  106.2 7.6 %collective-permute-start.29 = (f16[520,128]{1,0:T(8,128)(2,1)S(1)}, f16[520,128]{1,0:T(8,128)(2,1)S(1)}, u32[]{:S(2)}, u32[]{:S(2)}) collective-permute-start(f16[520,128]{1,0:T(8,128)(2,1)S(1)} %convert_element_type.17), channel_id=1, source_target_pairs={{0,64},{32,96},{64,0},{96,32},{1,65},{33,97},{65,1},{97,33},{2,66}... | collective-permute-start | bytes 399368 | tf_op jit(solution)/shard_map/ppermute | solution.py:488
  109.4 5.0 %collective-permute-start.30 = (f16[520,128]{1,0:T(8,128)(2,1)S(1)}, f16[520,128]{1,0:T(8,128)(2,1)S(1)}, u32[]{:S(2)}, u32[]{:S(2)}) collective-permute-start(f16[520,128]{1,0:T(8,128)(2,1)S(1)} %convert_element_type.17), channel_id=1, source_target_pairs={{0,96},{32,0},{64,32},{96,64},{1,97},{33,1},{65,33},{97,65},{2,98}... | collective-permute-start | bytes 399368 | tf_op jit(solution)/shard_map/ppermute | solution.py:488
  114.5 2.0 %collective-permute-start.31 = (f32[4,32,8,128]{3,2,1,0:T(8,128)S(1)}, f32[4,32,8,128]{3,2,1,0:T(8,128)S(1)}, u32[]{:S(2)}, u32[]{:S(2)}) collective-permute-start(f32[4,32,8,128]{3,2,1,0:T(8,128)S(1)} %shard_map.68), channel_id=1, source_target_pairs={{0,1},{1,0},{2,3},{3,2},{4,5},{5,4},{6,7},{7,6},{8,9},{9,8},{10,11... | collective-permute-start | bytes 1572872 | tf_op jit(solution)/shard_map/ppermute | solution.py:546
  (7 other events, 38.8 us)

commit v2 on v1

--- a/solution.py
+++ b/solution.py
@@ -506,9 +506,9 @@
         parts = call(back_y_kernel, [arr(quart, BF16)] * VIEWS, [flat])(
             far, ratio, near, yb, *(every[1:] if step == 0 else ())
         )
-        terms = [parts[0]] + [
-            lax.ppermute(parts[i], "view", steps(VIEWS, i)) for i in range(1, VIEWS)
-        ]
+        terms = [parts[0]]
+        for i in range(1, VIEWS):
+            terms.append(lax.ppermute(parts[i], "view", steps(VIEWS, i)))
         if step == 0:
             field, sent = call(
                 first_update_kernel,

time: 119 us -> 119 us (level)
  no operation moved by 1% of the time
where the time goes in v2:
time: 119 us; the launch traced here: 118 us
  starting transfers between devices  54.3 us (46%)
  waiting for transfers between devices  44.2 us (37%)
  Pallas kernels  16.6 us (14%)
  local copies, waits for them, and re-layouts  2.14 us (2%)
    ppermute x12, starting transfers between devices, from_views(): lax.ppermute(x, 'view', steps(VIEWS, i))  18.4 us
    ppermute x12, waiting for transfers between devices, from_views(): lax.ppermute(x, 'view', steps(VIEWS, i))  17.4 us
    pallas_call x15, Pallas kernels, run(): pl.pallas_call(kernel, out_shape=shapes, in_specs=specs, out_specs=[pl.Bl...  16.6 us
    ppermute x6, starting transfers between devices, on_device(): terms.append(lax.ppermute(parts[i], 'view', steps(VIEWS, i)))  9.62 us
    ppermute x6, waiting for transfers between devices, on_device(): terms.append(lax.ppermute(parts[i], 'view', steps(VIEWS, i)))  9.6 us
    ppermute x4, waiting for transfers between devices, neighbours(): return (lax.ppermute(x, STRIPS, across), lax.ppermute(x, 'gz', swap))  8.9 us
    ppermute x4, starting transfers between devices, neighbours(): return (lax.ppermute(x, STRIPS, across), lax.ppermute(x, 'gz', swap))  7.55 us
    ppermute x1, starting transfers between devices, on_device(): lax.ppermute(vm, STRIPS, inward)  5.86 us
  transfers between devices with their start and end apart: 32, of which 21 were waited for; matrix products, arithmetic and copies ran while one was open for 0% of the time, Pallas kernels for 5%

profile of v2, /device:TPU:0, one launch (start us, length us, event | category | flops | bytes accessed | tf_op | source)
XLA Modules:
  0.0 117.6 jit_solution(2199609950181814842)
XLA Ops:
  2.1 1.7 %collective-permute-start.4 = (bf16[32,32,128]{2,1,0:T(8,128)(2,1)S(1)}, bf16[32,32,128]{2,1,0:T(8,128)(2,1)S(1)}, u32[]{:S(2)}, u32[]{:S(2)}) collective-permute-start(bf16[32,32,128]{2,1,0:T(8,128)(2,1)S(1)} %get-tuple-element.42), channel_id=1, source_target_pairs={{0,2},{1,31},{2,4},{3,1},{4,6},{5,3},{6,8},{7,5},{8,10},{9,7},{10,... | collective-permute-start | bytes 786440 | tf_op jit(solution)/shard_map/ppermute | solution.py:447
  3.8 5.1 %collective-permute-start = (bf16[32,64,128]{2,1,0:T(8,128)(2,1)S(1)}, bf16[32,64,128]{2,1,0:T(8,128)(2,1)S(1)}, u32[]{:S(2)}, u32[]{:S(2)}) collective-permute-start(bf16[32,64,128]{2,1,0:T(8,128)(2,1)S(1)} %bitcast.6), channel_id=1, source_target_pairs={{0,1},{1,0},{2,3},{3,2},{4,5},{5,4},{6,7},{7,6},{8,9},{9,8},{10,11... | collective-permute-start | bytes 1572872 | tf_op jit(solution)/shard_map/ppermute | solution.py:449
  11.5 1.6 %collective-permute-done.4.far_a = bf16[32,32,128]{2,1,0:T(8,128)(2,1)S(1)} collective-permute-done((bf16[32,32,128]{2,1,0:T(8,128)(2,1)S(1)}, bf16[32,32,128]{2,1,0:T(8,128)(2,1)S(1)}, u32[]{:S(2)}, u32[]{:S(2)}) %collective-permute-start.4) | collective-permute-done | bytes 262176 | tf_op jit(solution)/shard_map/ppermute | solution.py:447
  13.1 5.9 %collective-permute-start.2 = (bf16[32,32,128]{2,1,0:T(8,128)(2,1)}, bf16[32,32,128]{2,1,0:T(8,128)(2,1)S(1)}, u32[]{:S(2)}, u32[]{:S(2)}) collective-permute-start(bf16[32,32,128]{2,1,0:T(8,128)(2,1)} %get-tuple-element.38), channel_id=1, source_target_pairs={{0,31},{1,2},{2,1},{3,4},{4,3},{5,6},{6,5},{7,8},{8,7},{9,10},{10,... | collective-permute-start | bytes 786440 | tf_op jit(solution)/shard_map/ppermute | solution.py:450
  20.5 2.3 %shard_map.58.pred = f32[2048,128]{1,0:T(8,128)S(1)} custom-call(bf16[32,64,128]{2,1,0:T(8,128)(2,1)S(1)} %get-tuple-element.41.slab, bf16[32,64,128]{2,1,0:T(8,128)(2,1)S(1)} %collective-permute-done.3.other, bf16[32,32,128]{2,1,0:T(8,128)(2,1)S(1)} %collective-permute-done.4.far_a, bf16[32,32,128]{2,1,0:T(8,128)(2,1)S(1)} %collective-permute-done.5.far_b, ...), custom_call_target="tpu_custom_call" | custom-call | flops 100000000 | bytes 4194304 | tf_op jit(solution)/shard_map/pallas_call | solution.py:46
  25.2 4.4 %collective-permute-start.6 = (bf16[64,32,128]{2,1,0:T(8,128)(2,1)S(1)}, bf16[64,32,128]{2,1,0:T(8,128)(2,1)S(1)}, u32[]{:S(2)}, u32[]{:S(2)}) collective-permute-start(bf16[64,32,128]{2,1,0:T(8,128)(2,1)S(1)} %get-tuple-element.48.own), channel_id=1, source_target_pairs={{0,31},{1,2},{2,1},{3,4},{4,3},{5,6},{6,5},{7,8},{8,7},{9,10},{10,... | collective-permute-start | bytes 1572872 | tf_op jit(solution)/shard_map/ppermute | solution.py:485
  29.7 2.8 %collective-permute-start.10 = (f32[8,128]{1,0:T(8,128)S(1)}, f32[8,128]{1,0:T(8,128)S(1)}, u32[]{:S(2)}, u32[]{:S(2)}) collective-permute-start(f32[8,128]{1,0:T(8,128)S(1)} %select_maximum_fusion.taps.t0), channel_id=1, source_target_pairs={{0,96},{32,0},{64,32},{96,64},{1,97},{33,1},{65,33},{97,65},{2,98}... | collective-permute-start | bytes 12296 | tf_op jit(solution)/shard_map/ppermute | solution.py:488
  32.4 2.3 %collective-permute-start.9 = (f32[8,128]{1,0:T(8,128)S(1)}, f32[8,128]{1,0:T(8,128)S(1)}, u32[]{:S(2)}, u32[]{:S(2)}) collective-permute-start(f32[8,128]{1,0:T(8,128)S(1)} %select_maximum_fusion.taps.t0), channel_id=1, source_target_pairs={{0,64},{32,96},{64,0},{96,32},{1,65},{33,97},{65,1},{97,33},{2,66}... | collective-permute-start | bytes 12296 | tf_op jit(solution)/shard_map/ppermute | solution.py:488
  34.7 2.5 %collective-permute-done.8.refs_0_.t1 = f32[8,128]{1,0:T(8,128)S(1)} collective-permute-done((f32[8,128]{1,0:T(8,128)S(1)}, f32[8,128]{1,0:T(8,128)S(1)}, u32[]{:S(2)}, u32[]{:S(2)}) %collective-permute-start.8) | collective-permute-done | bytes 4128 | tf_op jit(solution)/shard_map/ppermute | solution.py:488
  39.8 3.5 %collective-permute-start.12 = (bf16[512,128]{1,0:T(8,128)(2,1)S(1)}, bf16[512,128]{1,0:T(8,128)(2,1)S(1)}, u32[]{:S(2)}, u32[]{:S(2)}) collective-permute-start(bf16[512,128]{1,0:T(8,128)(2,1)S(1)} %get-tuple-element.54), channel_id=1, source_target_pairs={{0,64},{32,96},{64,0},{96,32},{1,65},{33,97},{65,1},{97,33},{2,66}... | collective-permute-start | bytes 393224 | tf_op jit(solution)/shard_map/ppermute | solution.py:511
  45.7 2.9 %collective-permute-done.12.t2 = bf16[512,128]{1,0:T(8,128)(2,1)S(1)} collective-permute-done((bf16[512,128]{1,0:T(8,128)(2,1)S(1)}, bf16[512,128]{1,0:T(8,128)(2,1)S(1)}, u32[]{:S(2)}, u32[]{:S(2)}) %collective-permute-start.12) | collective-permute-done | bytes 131104 | tf_op jit(solution)/shard_map/ppermute | solution.py:511
  48.6 1.8 %shard_map.62 = (f32[512,128]{1,0:T(8,128)S(1)}, bf16[64,8,128]{2,1,0:T(8,128)(2,1)S(1)}) custom-call(bf16[512,128]{1,0:T(8,128)(2,1)S(1)} %get-tuple-element.52.t0, bf16[512,128]{1,0:T(8,128)(2,1)S(1)} %collective-permute-done.11.t1, bf16[512,128]{1,0:T(8,128)(2,1)S(1)} %collective-permute-done.12.t2, bf16[512,128]{1,0:T(8,128)(2,1)S(1)} %collective-permute-done.13.t3, ...), custom_call_target="tpu_custom_call" | custom-call | flops 100000000 | bytes 4194304 | tf_op jit(solution)/shard_map/pallas_call | solution.py:46
  51.2 2.8 %collective-permute-start.20 = (bf16[64,8,128]{2,1,0:T(8,128)(2,1)S(1)}, bf16[64,8,128]{2,1,0:T(8,128)(2,1)S(1)}, u32[]{:S(2)}, u32[]{:S(2)}) collective-permute-start(bf16[64,8,128]{2,1,0:T(8,128)(2,1)S(1)} %get-tuple-element.61.p0.sent.s0), channel_id=1, source_target_pairs={{0,64},{32,96},{64,0},{96,32},{1,65},{33,97},{65,1},{97,33},{2,66}... | collective-permute-start | bytes 393224 | tf_op jit(solution)/shard_map/ppermute | solution.py:488
  54.5 2.9 %collective-permute-done.19.p1.s1 = bf16[64,8,128]{2,1,0:T(8,128)(2,1)S(1)} collective-permute-done((bf16[64,8,128]{2,1,0:T(8,128)(2,1)S(1)}, bf16[64,8,128]{2,1,0:T(8,128)(2,1)S(1)}, u32[]{:S(2)}, u32[]{:S(2)}) %collective-permute-start.19) | collective-permute-done | bytes 131104 | tf_op jit(solution)/shard_map/ppermute | solution.py:488
  59.5 4.2 %collective-permute-start.15 = (bf16[64,8,128]{2,1,0:T(8,128)(2,1)S(1)}, bf16[64,8,128]{2,1,0:T(8,128)(2,1)S(1)}, u32[]{:S(2)}, u32[]{:S(2)}) collective-permute-start(bf16[64,8,128]{2,1,0:T(8,128)(2,1)S(1)} %get-tuple-element.61.p0.sent.s0), channel_id=1, source_target_pairs={{0,31},{1,2},{2,1},{3,4},{4,3},{5,6},{6,5},{7,8},{8,7},{9,10},{10,... | collective-permute-start | bytes 393224 | tf_op jit(solution)/shard_map/ppermute | solution.py:527
  63.8 3.7 %collective-permute-done.15.p0 = bf16[64,8,128]{2,1,0:T(8,128)(2,1)S(1)} collective-permute-done((bf16[64,8,128]{2,1,0:T(8,128)(2,1)S(1)}, bf16[64,8,128]{2,1,0:T(8,128)(2,1)S(1)}, u32[]{:S(2)}, u32[]{:S(2)}) %collective-permute-start.15) | collective-permute-done | bytes 131104 | tf_op jit(solution)/shard_map/ppermute | solution.py:527
  68.2 3.4 %collective-permute-start.17 = (bf16[64,8,128]{2,1,0:T(8,128)(2,1)S(1)}, bf16[64,8,128]{2,1,0:T(8,128)(2,1)S(1)}, u32[]{:S(2)}, u32[]{:S(2)}) collective-permute-start(bf16[64,8,128]{2,1,0:T(8,128)(2,1)S(1)} %collective-permute-done.15.p0), channel_id=1, source_target_pairs={{0,64},{32,96},{64,0},{96,32},{1,65},{33,97},{65,1},{97,33},{2,66}... | collective-permute-start | bytes 393224 | tf_op jit(solution)/shard_map/ppermute | solution.py:488
  71.6 2.0 %collective-permute-done.16.p1 = bf16[64,8,128]{2,1,0:T(8,128)(2,1)S(1)} collective-permute-done((bf16[64,8,128]{2,1,0:T(8,128)(2,1)S(1)}, bf16[64,8,128]{2,1,0:T(8,128)(2,1)S(1)}, u32[]{:S(2)}, u32[]{:S(2)}) %collective-permute-start.16) | collective-permute-done | bytes 131104 | tf_op jit(solution)/shard_map/ppermute | solution.py:488
  73.7 2.3 %collective-permute-done.17.p2 = bf16[64,8,128]{2,1,0:T(8,128)(2,1)S(1)} collective-permute-done((bf16[64,8,128]{2,1,0:T(8,128)(2,1)S(1)}, bf16[64,8,128]{2,1,0:T(8,128)(2,1)S(1)}, u32[]{:S(2)}, u32[]{:S(2)}) %collective-permute-start.17) | collective-permute-done | bytes 131104 | tf_op jit(solution)/shard_map/ppermute | solution.py:488
  76.8 2.2 %shard_map.65.own = bf16[64,32,128]{2,1,0:T(8,128)(2,1)S(1)} custom-call(bf16[64,32,128]{2,1,0:T(8,128)(2,1)S(1)} %shard_map.63.far, bf16[64,32,128]{2,1,0:T(8,128)(2,1)S(1)} %shard_map.64.own, bf16[64,32,128]{2,1,0:T(8,128)(2,1)S(1)} %collective-permute-done.22.near, bf16[64,128]{1,0:T(8,128)(2,1)S(1)} %get-tuple-element.62.yf, ...), custom_call_target="tpu_custom_call" | custom-call | flops 100000000 | bytes 4194304 | tf_op jit(solution)/shard_map/pallas_call | solution.py:46
  79.0 3.1 %collective-permute-start.23 = (bf16[64,32,128]{2,1,0:T(8,128)(2,1)S(1)}, bf16[64,32,128]{2,1,0:T(8,128)(2,1)S(1)}, u32[]{:S(2)}, u32[]{:S(2)}) collective-permute-start(bf16[64,32,128]{2,1,0:T(8,128)(2,1)S(1)} %shard_map.65.own), channel_id=1, source_target_pairs={{0,31},{1,2},{2,1},{3,4},{4,3},{5,6},{6,5},{7,8},{8,7},{9,10},{10,... | collective-permute-start | bytes 1572872 | tf_op jit(solution)/shard_map/ppermute | solution.py:485
  82.1 8.9 %collective-permute-done.23.far = bf16[64,32,128]{2,1,0:T(8,128)(2,1)S(1)} collective-permute-done((bf16[64,32,128]{2,1,0:T(8,128)(2,1)S(1)}, bf16[64,32,128]{2,1,0:T(8,128)(2,1)S(1)}, u32[]{:S(2)}, u32[]{:S(2)}) %collective-permute-start.23) | collective-permute-done | bytes 524320 | tf_op jit(solution)/shard_map/ppermute | solution.py:485
  92.2 3.4 %collective-permute-start.26 = (bf16[512,128]{1,0:T(8,128)(2,1)S(1)}, bf16[512,128]{1,0:T(8,128)(2,1)S(1)}, u32[]{:S(2)}, u32[]{:S(2)}) collective-permute-start(bf16[512,128]{1,0:T(8,128)(2,1)S(1)} %get-tuple-element.66), channel_id=1, source_target_pairs={{0,64},{32,96},{64,0},{96,32},{1,65},{33,97},{65,1},{97,33},{2,66}... | collective-permute-start | bytes 393224 | tf_op jit(solution)/shard_map/ppermute | solution.py:511
  96.2 2.2 %collective-permute-done.25.t1 = bf16[512,128]{1,0:T(8,128)(2,1)S(1)} collective-permute-done((bf16[512,128]{1,0:T(8,128)(2,1)S(1)}, bf16[512,128]{1,0:T(8,128)(2,1)S(1)}, u32[]{:S(2)}, u32[]{:S(2)}) %collective-permute-start.25) | collective-permute-done | bytes 131104 | tf_op jit(solution)/shard_map/ppermute | solution.py:511
  98.4 2.4 %collective-permute-done.26.t2 = bf16[512,128]{1,0:T(8,128)(2,1)S(1)} collective-permute-done((bf16[512,128]{1,0:T(8,128)(2,1)S(1)}, bf16[512,128]{1,0:T(8,128)(2,1)S(1)}, u32[]{:S(2)}, u32[]{:S(2)}) %collective-permute-start.26) | collective-permute-done | bytes 131104 | tf_op jit(solution)/shard_map/ppermute | solution.py:511
  100.9 1.5 %collective-permute-done.27.t3 = bf16[512,128]{1,0:T(8,128)(2,1)S(1)} collective-permute-done((bf16[512,128]{1,0:T(8,128)(2,1)S(1)}, bf16[512,128]{1,0:T(8,128)(2,1)S(1)}, u32[]{:S(2)}, u32[]{:S(2)}) %collective-permute-start.27) | collective-permute-done | bytes 131104 | tf_op jit(solution)/shard_map/ppermute | solution.py:511
  102.4 1.9 %shard_map.67 = f32[520,128]{1,0:T(8,128)S(1)} custom-call(bf16[512,128]{1,0:T(8,128)(2,1)S(1)} %get-tuple-element.64.t0, bf16[512,128]{1,0:T(8,128)(2,1)S(1)} %collective-permute-done.25.t1, bf16[512,128]{1,0:T(8,128)(2,1)S(1)} %collective-permute-done.26.t2, bf16[512,128]{1,0:T(8,128)(2,1)S(1)} %collective-permute-done.27.t3, ...), custom_call_target="tpu_custom_call" | custom-call | flops 100000000 | bytes 4194304 | tf_op jit(solution)/shard_map/pallas_call | solution.py:46
  104.3 1.9 %collective-permute-start.28 = (f16[520,128]{1,0:T(8,128)(2,1)S(1)}, f16[520,128]{1,0:T(8,128)(2,1)S(1)}, u32[]{:S(2)}, u32[]{:S(2)}) collective-permute-start(f16[520,128]{1,0:T(8,128)(2,1)S(1)} %convert_element_type.17), channel_id=1, source_target_pairs={{0,32},{32,64},{64,96},{96,0},{1,33},{33,65},{65,97},{97,1},{2,34}... | collective-permute-start | bytes 399368 | tf_op jit(solution)/shard_map/ppermute | solution.py:488
  106.2 3.2 %collective-permute-start.29 = (f16[520,128]{1,0:T(8,128)(2,1)S(1)}, f16[520,128]{1,0:T(8,128)(2,1)S(1)}, u32[]{:S(2)}, u32[]{:S(2)}) collective-permute-start(f16[520,128]{1,0:T(8,128)(2,1)S(1)} %convert_element_type.17), channel_id=1, source_target_pairs={{0,64},{32,96},{64,0},{96,32},{1,65},{33,97},{65,1},{97,33},{2,66}... | collective-permute-start | bytes 399368 | tf_op jit(solution)/shard_map/ppermute | solution.py:488
  109.4 1.5 %collective-permute-done.28 = f16[520,128]{1,0:T(8,128)(2,1)S(1)} collective-permute-done((f16[520,128]{1,0:T(8,128)(2,1)S(1)}, f16[520,128]{1,0:T(8,128)(2,1)S(1)}, u32[]{:S(2)}, u32[]{:S(2)}) %collective-permute-start.28) | collective-permute-done | bytes 133152 | tf_op jit(solution)/shard_map/ppermute | solution.py:488
  110.9 2.9 %collective-permute-done.29 = f16[520,128]{1,0:T(8,128)(2,1)S(1)} collective-permute-done((f16[520,128]{1,0:T(8,128)(2,1)S(1)}, f16[520,128]{1,0:T(8,128)(2,1)S(1)}, u32[]{:S(2)}, u32[]{:S(2)}) %collective-permute-start.29) | collective-permute-done | bytes 133152 | tf_op jit(solution)/shard_map/ppermute | solution.py:488
  114.6 1.9 %collective-permute-done.31.got = f32[4,32,8,128]{3,2,1,0:T(8,128)S(1)} collective-permute-done((f32[4,32,8,128]{3,2,1,0:T(8,128)S(1)}, f32[4,32,8,128]{3,2,1,0:T(8,128)S(1)}, u32[]{:S(2)}, u32[]{:S(2)}) %collective-permute-start.31) | collective-permute-done | bytes 524320 | tf_op jit(solution)/shard_map/ppermute | solution.py:546
  (70 shorter events, 22.3 us)
Async XLA Ops:
  2.1 18.4 %collective-permute-start.3 = (bf16[32,64,128]{2,1,0:T(8,128)(2,1)S(1)}, bf16[32,64,128]{2,1,0:T(8,128)(2,1)S(1)}, u32[]{:S(2)}, u32[]{:S(2)}) collective-permute-start(bf16[32,64,128]{2,1,0:T(8,128)(2,1)S(1)} %get-tuple-element.41.slab), channel_id=1, source_target_pairs={{0,1},{1,0},{2,3},{3,2},{4,5},{5,4},{6,7},{7,6},{8,9},{9,8},{10,11... | collective-permute-start | bytes 1572872 | tf_op jit(solution)/shard_map/ppermute | solution.py:448
  2.1 10.9 %collective-permute-start.4 = (bf16[32,32,128]{2,1,0:T(8,128)(2,1)S(1)}, bf16[32,32,128]{2,1,0:T(8,128)(2,1)S(1)}, u32[]{:S(2)}, u32[]{:S(2)}) collective-permute-start(bf16[32,32,128]{2,1,0:T(8,128)(2,1)S(1)} %get-tuple-element.42), channel_id=1, source_target_pairs={{0,2},{1,31},{2,4},{3,1},{4,6},{5,3},{6,8},{7,5},{8,10},{9,7},{10,... | collective-permute-start | bytes 786440 | tf_op jit(solution)/shard_map/ppermute | solution.py:447
  3.8 20.1 %collective-permute-start = (bf16[32,64,128]{2,1,0:T(8,128)(2,1)S(1)}, bf16[32,64,128]{2,1,0:T(8,128)(2,1)S(1)}, u32[]{:S(2)}, u32[]{:S(2)}) collective-permute-start(bf16[32,64,128]{2,1,0:T(8,128)(2,1)S(1)} %bitcast.6), channel_id=1, source_target_pairs={{0,1},{1,0},{2,3},{3,2},{4,5},{5,4},{6,7},{7,6},{8,9},{9,8},{10,11... | collective-permute-start | bytes 1572872 | tf_op jit(solution)/shard_map/ppermute | solution.py:449
  9.0 11.5 %collective-permute-start.5 = (bf16[32,32,128]{2,1,0:T(8,128)(2,1)}, bf16[32,32,128]{2,1,0:T(8,128)(2,1)S(1)}, u32[]{:S(2)}, u32[]{:S(2)}) collective-permute-start(bf16[32,32,128]{2,1,0:T(8,128)(2,1)} %get-tuple-element.43), channel_id=1, source_target_pairs={{0,31},{1,2},{2,1},{3,4},{4,3},{5,6},{6,5},{7,8},{8,7},{9,10},{10,... | collective-permute-start | bytes 786440 | tf_op jit(solution)/shard_map/ppermute | solution.py:447
  10.2 12.6 %collective-permute-start.1 = (bf16[32,32,128]{2,1,0:T(8,128)(2,1)}, bf16[32,32,128]{2,1,0:T(8,128)(2,1)S(1)}, u32[]{:S(2)}, u32[]{:S(2)}) collective-permute-start(bf16[32,32,128]{2,1,0:T(8,128)(2,1)} %get-tuple-element.37), channel_id=1, source_target_pairs={{0,2},{1,31},{2,4},{3,1},{4,6},{5,3},{6,8},{7,5},{8,10},{9,7},{10,... | collective-permute-start | bytes 786440 | tf_op jit(solution)/shard_map/ppermute | solution.py:450
  13.1 10.8 %collective-permute-start.2 = (bf16[32,32,128]{2,1,0:T(8,128)(2,1)}, bf16[32,32,128]{2,1,0:T(8,128)(2,1)S(1)}, u32[]{:S(2)}, u32[]{:S(2)}) collective-permute-start(bf16[32,32,128]{2,1,0:T(8,128)(2,1)} %get-tuple-element.38), channel_id=1, source_target_pairs={{0,31},{1,2},{2,1},{3,4},{4,3},{5,6},{6,5},{7,8},{8,7},{9,10},{10,... | collective-permute-start | bytes 786440 | tf_op jit(solution)/shard_map/ppermute | solution.py:450
  25.2 12.3 %collective-permute-start.6 = (bf16[64,32,128]{2,1,0:T(8,128)(2,1)S(1)}, bf16[64,32,128]{2,1,0:T(8,128)(2,1)S(1)}, u32[]{:S(2)}, u32[]{:S(2)}) collective-permute-start(bf16[64,32,128]{2,1,0:T(8,128)(2,1)S(1)} %get-tuple-element.48.own), channel_id=1, source_target_pairs={{0,31},{1,2},{2,1},{3,4},{4,3},{5,6},{6,5},{7,8},{8,7},{9,10},{10,... | collective-permute-start | bytes 1572872 | tf_op jit(solution)/shard_map/ppermute | solution.py:485
  29.7 7.9 %collective-permute-start.7 = (bf16[64,32,128]{2,1,0:T(8,128)(2,1)S(1)}, bf16[64,32,128]{2,1,0:T(8,128)(2,1)S(1)}, u32[]{:S(2)}, u32[]{:S(2)}) collective-permute-start(bf16[64,32,128]{2,1,0:T(8,128)(2,1)S(1)} %get-tuple-element.48.own), channel_id=1, source_target_pairs={{0,1},{1,0},{2,3},{3,2},{4,5},{5,4},{6,7},{7,6},{8,9},{9,8},{10,11... | collective-permute-start | bytes 1572872 | tf_op jit(solution)/shard_map/ppermute | solution.py:485
  29.7 5.0 %collective-permute-start.10 = (f32[8,128]{1,0:T(8,128)S(1)}, f32[8,128]{1,0:T(8,128)S(1)}, u32[]{:S(2)}, u32[]{:S(2)}) collective-permute-start(f32[8,128]{1,0:T(8,128)S(1)} %select_maximum_fusion.taps.t0), channel_id=1, source_target_pairs={{0,96},{32,0},{64,32},{96,64},{1,97},{33,1},{65,33},{97,65},{2,98}... | collective-permute-start | bytes 12296 | tf_op jit(solution)/shard_map/ppermute | solution.py:488
  32.4 4.8 %collective-permute-start.8 = (f32[8,128]{1,0:T(8,128)S(1)}, f32[8,128]{1,0:T(8,128)S(1)}, u32[]{:S(2)}, u32[]{:S(2)}) collective-permute-start(f32[8,128]{1,0:T(8,128)S(1)} %select_maximum_fusion.taps.t0), channel_id=1, source_target_pairs={{0,32},{32,64},{64,96},{96,0},{1,33},{33,65},{65,97},{97,1},{2,34}... | collective-permute-start | bytes 12296 | tf_op jit(solution)/shard_map/ppermute | solution.py:488
  32.4 5.1 %collective-permute-start.9 = (f32[8,128]{1,0:T(8,128)S(1)}, f32[8,128]{1,0:T(8,128)S(1)}, u32[]{:S(2)}, u32[]{:S(2)}) collective-permute-start(f32[8,128]{1,0:T(8,128)S(1)} %select_maximum_fusion.taps.t0), channel_id=1, source_target_pairs={{0,64},{32,96},{64,0},{96,32},{1,65},{33,97},{65,1},{97,33},{2,66}... | collective-permute-start | bytes 12296 | tf_op jit(solution)/shard_map/ppermute | solution.py:488
  34.7 10.4 %collective-permute-start.14 = (f32[32,8,128]{2,1,0:T(8,128)S(1)}, f32[32,8,128]{2,1,0:T(8,128)S(1)}, u32[]{:S(2)}, u32[]{:S(2)}) collective-permute-start(f32[32,8,128]{2,1,0:T(8,128)S(1)} %copy-done.4), channel_id=1, source_target_pairs={{0,1},{1,0},{2,3},{3,2},{4,5},{5,4},{6,7},{7,6},{8,9},{9,8},{10,11... | collective-permute-start | bytes 393224 | tf_op jit(solution)/shard_map/ppermute | solution.py:491
  38.6 7.1 %collective-permute-start.11 = (bf16[512,128]{1,0:T(8,128)(2,1)S(1)}, bf16[512,128]{1,0:T(8,128)(2,1)S(1)}, u32[]{:S(2)}, u32[]{:S(2)}) collective-permute-start(bf16[512,128]{1,0:T(8,128)(2,1)S(1)} %get-tuple-element.53), channel_id=1, source_target_pairs={{0,32},{32,64},{64,96},{96,0},{1,33},{33,65},{65,97},{97,1},{2,34}... | collective-permute-start | bytes 393224 | tf_op jit(solution)/shard_map/ppermute | solution.py:511
  39.8 8.8 %collective-permute-start.12 = (bf16[512,128]{1,0:T(8,128)(2,1)S(1)}, bf16[512,128]{1,0:T(8,128)(2,1)S(1)}, u32[]{:S(2)}, u32[]{:S(2)}) collective-permute-start(bf16[512,128]{1,0:T(8,128)(2,1)S(1)} %get-tuple-element.54), channel_id=1, source_target_pairs={{0,64},{32,96},{64,0},{96,32},{1,65},{33,97},{65,1},{97,33},{2,66}... | collective-permute-start | bytes 393224 | tf_op jit(solution)/shard_map/ppermute | solution.py:511
  43.3 5.3 %collective-permute-start.13 = (bf16[512,128]{1,0:T(8,128)(2,1)S(1)}, bf16[512,128]{1,0:T(8,128)(2,1)S(1)}, u32[]{:S(2)}, u32[]{:S(2)}) collective-permute-start(bf16[512,128]{1,0:T(8,128)(2,1)S(1)} %get-tuple-element.55), channel_id=1, source_target_pairs={{0,96},{32,0},{64,32},{96,64},{1,97},{33,1},{65,33},{97,65},{2,98}... | collective-permute-start | bytes 393224 | tf_op jit(solution)/shard_map/ppermute | solution.py:511
  50.4 7.0 %collective-permute-start.19 = (bf16[64,8,128]{2,1,0:T(8,128)(2,1)S(1)}, bf16[64,8,128]{2,1,0:T(8,128)(2,1)S(1)}, u32[]{:S(2)}, u32[]{:S(2)}) collective-permute-start(bf16[64,8,128]{2,1,0:T(8,128)(2,1)S(1)} %get-tuple-element.61.p0.sent.s0), channel_id=1, source_target_pairs={{0,32},{32,64},{64,96},{96,0},{1,33},{33,65},{65,97},{97,1},{2,34}... | collective-permute-start | bytes 393224 | tf_op jit(solution)/shard_map/ppermute | solution.py:488
  51.2 7.6 %collective-permute-start.20 = (bf16[64,8,128]{2,1,0:T(8,128)(2,1)S(1)}, bf16[64,8,128]{2,1,0:T(8,128)(2,1)S(1)}, u32[]{:S(2)}, u32[]{:S(2)}) collective-permute-start(bf16[64,8,128]{2,1,0:T(8,128)(2,1)S(1)} %get-tuple-element.61.p0.sent.s0), channel_id=1, source_target_pairs={{0,64},{32,96},{64,0},{96,32},{1,65},{33,97},{65,1},{97,33},{2,66}... | collective-permute-start | bytes 393224 | tf_op jit(solution)/shard_map/ppermute | solution.py:488
  54.0 5.1 %collective-permute-start.21 = (bf16[64,8,128]{2,1,0:T(8,128)(2,1)S(1)}, bf16[64,8,128]{2,1,0:T(8,128)(2,1)S(1)}, u32[]{:S(2)}, u32[]{:S(2)}) collective-permute-start(bf16[64,8,128]{2,1,0:T(8,128)(2,1)S(1)} %get-tuple-element.61.p0.sent.s0), channel_id=1, source_target_pairs={{0,96},{32,0},{64,32},{96,64},{1,97},{33,1},{65,33},{97,65},{2,98}... | collective-permute-start | bytes 393224 | tf_op jit(solution)/shard_map/ppermute | solution.py:488
  59.4 17.4 %collective-permute-start.22 = (bf16[64,32,128]{2,1,0:T(8,128)(2,1)S(1)}, bf16[64,32,128]{2,1,0:T(8,128)(2,1)S(1)}, u32[]{:S(2)}, u32[]{:S(2)}) collective-permute-start(bf16[64,32,128]{2,1,0:T(8,128)(2,1)S(1)} %shard_map.64.own), channel_id=1, source_target_pairs={{0,1},{1,0},{2,3},{3,2},{4,5},{5,4},{6,7},{7,6},{8,9},{9,8},{10,11... | collective-permute-start | bytes 1572872 | tf_op jit(solution)/shard_map/ppermute | solution.py:531
  59.5 8.0 %collective-permute-start.15 = (bf16[64,8,128]{2,1,0:T(8,128)(2,1)S(1)}, bf16[64,8,128]{2,1,0:T(8,128)(2,1)S(1)}, u32[]{:S(2)}, u32[]{:S(2)}) collective-permute-start(bf16[64,8,128]{2,1,0:T(8,128)(2,1)S(1)} %get-tuple-element.61.p0.sent.s0), channel_id=1, source_target_pairs={{0,31},{1,2},{2,1},{3,4},{4,3},{5,6},{6,5},{7,8},{8,7},{9,10},{10,... | collective-permute-start | bytes 393224 | tf_op jit(solution)/shard_map/ppermute | solution.py:527
  67.5 6.2 %collective-permute-start.16 = (bf16[64,8,128]{2,1,0:T(8,128)(2,1)S(1)}, bf16[64,8,128]{2,1,0:T(8,128)(2,1)S(1)}, u32[]{:S(2)}, u32[]{:S(2)}) collective-permute-start(bf16[64,8,128]{2,1,0:T(8,128)(2,1)S(1)} %collective-permute-done.15.p0), channel_id=1, source_target_pairs={{0,32},{32,64},{64,96},{96,0},{1,33},{33,65},{65,97},{97,1},{2,34}... | collective-permute-start | bytes 393224 | tf_op jit(solution)/shard_map/ppermute | solution.py:488
  68.2 7.7 %collective-permute-start.17 = (bf16[64,8,128]{2,1,0:T(8,128)(2,1)S(1)}, bf16[64,8,128]{2,1,0:T(8,128)(2,1)S(1)}, u32[]{:S(2)}, u32[]{:S(2)}) collective-permute-start(bf16[64,8,128]{2,1,0:T(8,128)(2,1)S(1)} %collective-permute-done.15.p0), channel_id=1, source_target_pairs={{0,64},{32,96},{64,0},{96,32},{1,65},{33,97},{65,1},{97,33},{2,66}... | collective-permute-start | bytes 393224 | tf_op jit(solution)/shard_map/ppermute | solution.py:488
  71.6 5.0 %collective-permute-start.18 = (bf16[64,8,128]{2,1,0:T(8,128)(2,1)S(1)}, bf16[64,8,128]{2,1,0:T(8,128)(2,1)S(1)}, u32[]{:S(2)}, u32[]{:S(2)}) collective-permute-start(bf16[64,8,128]{2,1,0:T(8,128)(2,1)S(1)} %collective-permute-done.15.p0), channel_id=1, source_target_pairs={{0,96},{32,0},{64,32},{96,64},{1,97},{33,1},{65,33},{97,65},{2,98}... | collective-permute-start | bytes 393224 | tf_op jit(solution)/shard_map/ppermute | solution.py:488
  79.0 12.0 %collective-permute-start.23 = (bf16[64,32,128]{2,1,0:T(8,128)(2,1)S(1)}, bf16[64,32,128]{2,1,0:T(8,128)(2,1)S(1)}, u32[]{:S(2)}, u32[]{:S(2)}) collective-permute-start(bf16[64,32,128]{2,1,0:T(8,128)(2,1)S(1)} %shard_map.65.own), channel_id=1, source_target_pairs={{0,31},{1,2},{2,1},{3,4},{4,3},{5,6},{6,5},{7,8},{8,7},{9,10},{10,... | collective-permute-start | bytes 1572872 | tf_op jit(solution)/shard_map/ppermute | solution.py:485
  82.1 8.9 %collective-permute-start.24 = (bf16[64,32,128]{2,1,0:T(8,128)(2,1)S(1)}, bf16[64,32,128]{2,1,0:T(8,128)(2,1)S(1)}, u32[]{:S(2)}, u32[]{:S(2)}) collective-permute-start(bf16[64,32,128]{2,1,0:T(8,128)(2,1)S(1)} %shard_map.65.own), channel_id=1, source_target_pairs={{0,1},{1,0},{2,3},{3,2},{4,5},{5,4},{6,7},{7,6},{8,9},{9,8},{10,11... | collective-permute-start | bytes 1572872 | tf_op jit(solution)/shard_map/ppermute | solution.py:485
  92.0 6.4 %collective-permute-start.25 = (bf16[512,128]{1,0:T(8,128)(2,1)S(1)}, bf16[512,128]{1,0:T(8,128)(2,1)S(1)}, u32[]{:S(2)}, u32[]{:S(2)}) collective-permute-start(bf16[512,128]{1,0:T(8,128)(2,1)S(1)} %get-tuple-element.65), channel_id=1, source_target_pairs={{0,32},{32,64},{64,96},{96,0},{1,33},{33,65},{65,97},{97,1},{2,34}... | collective-permute-start | bytes 393224 | tf_op jit(solution)/shard_map/ppermute | solution.py:511
  92.2 8.7 %collective-permute-start.26 = (bf16[512,128]{1,0:T(8,128)(2,1)S(1)}, bf16[512,128]{1,0:T(8,128)(2,1)S(1)}, u32[]{:S(2)}, u32[]{:S(2)}) collective-permute-start(bf16[512,128]{1,0:T(8,128)(2,1)S(1)} %get-tuple-element.66), channel_id=1, source_target_pairs={{0,64},{32,96},{64,0},{96,32},{1,65},{33,97},{65,1},{97,33},{2,66}... | collective-permute-start | bytes 393224 | tf_op jit(solution)/shard_map/ppermute | solution.py:511
  95.5 6.8 %collective-permute-start.27 = (bf16[512,128]{1,0:T(8,128)(2,1)S(1)}, bf16[512,128]{1,0:T(8,128)(2,1)S(1)}, u32[]{:S(2)}, u32[]{:S(2)}) collective-permute-start(bf16[512,128]{1,0:T(8,128)(2,1)S(1)} %get-tuple-element.67), channel_id=1, source_target_pairs={{0,96},{32,0},{64,32},{96,64},{1,97},{33,1},{65,33},{97,65},{2,98}... | collective-permute-start | bytes 393224 | tf_op jit(solution)/shard_map/ppermute | solution.py:511
  104.3 6.6 %collective-permute-start.28 = (f16[520,128]{1,0:T(8,128)(2,1)S(1)}, f16[520,128]{1,0:T(8,128)(2,1)S(1)}, u32[]{:S(2)}, u32[]{:S(2)}) collective-permute-start(f16[520,128]{1,0:T(8,128)(2,1)S(1)} %convert_element_type.17), channel_id=1, source_target_pairs={{0,32},{32,64},{64,96},{96,0},{1,33},{33,65},{65,97},{97,1},{2,34}... | collective-permute-start | bytes 399368 | tf_op jit(solution)/shard_map/ppermute | solution.py:488
  106.2 7.6 %collective-permute-start.29 = (f16[520,128]{1,0:T(8,128)(2,1)S(1)}, f16[520,128]{1,0:T(8,128)(2,1)S(1)}, u32[]{:S(2)}, u32[]{:S(2)}) collective-permute-start(f16[520,128]{1,0:T(8,128)(2,1)S(1)} %convert_element_type.17), channel_id=1, source_target_pairs={{0,64},{32,96},{64,0},{96,32},{1,65},{33,97},{65,1},{97,33},{2,66}... | collective-permute-start | bytes 399368 | tf_op jit(solution)/shard_map/ppermute | solution.py:488
  109.4 5.0 %collective-permute-start.30 = (f16[520,128]{1,0:T(8,128)(2,1)S(1)}, f16[520,128]{1,0:T(8,128)(2,1)S(1)}, u32[]{:S(2)}, u32[]{:S(2)}) collective-permute-start(f16[520,128]{1,0:T(8,128)(2,1)S(1)} %convert_element_type.17), channel_id=1, source_target_pairs={{0,96},{32,0},{64,32},{96,64},{1,97},{33,1},{65,33},{97,65},{2,98}... | collective-permute-start | bytes 399368 | tf_op jit(solution)/shard_map/ppermute | solution.py:488
  114.5 2.0 %collective-permute-start.31 = (f32[4,32,8,128]{3,2,1,0:T(8,128)S(1)}, f32[4,32,8,128]{3,2,1,0:T(8,128)S(1)}, u32[]{:S(2)}, u32[]{:S(2)}) collective-permute-start(f32[4,32,8,128]{3,2,1,0:T(8,128)S(1)} %shard_map.68), channel_id=1, source_target_pairs={{0,1},{1,0},{2,3},{3,2},{4,5},{5,4},{6,7},{7,6},{8,9},{9,8},{10,11... | collective-permute-start | bytes 1572872 | tf_op jit(solution)/shard_map/ppermute | solution.py:546
  (7 other events, 38.8 us)
